TPU v7x, 128 devices: a whole 4x4x4 slice. The times are simulated.
128 devices in a mesh: req: 16 (over x, z), kv: 8 (over y, core).
Axes of the slice: x: 4, y: 4, z: 4, core: 2. Of those that a mesh axis runs over, the one named last changes fastest.
Arguments:
- residual_in: bfloat16 [512, 4096], P(None, 'req'), may hold values from -6 to 6
- attn_gain: float32 [4096], replicated, may hold values from 0.1 to 1.9
- query_weight: bfloat16 [4096, 4096], P(None, 'kv'), may hold values from -0.09375 to 0.09375
- key_matrix: bfloat16 [4096, 1024], P(None, 'kv'), may hold values from -0.09375 to 0.09375
- value_matrix: bfloat16 [4096, 1024], P(None, 'kv'), may hold values from -0.09375 to 0.09375
- key_cache: bfloat16 [512, 8, 640, 128], P('req', 'kv'), may hold values from -400 to 400
- cached_values: bfloat16 [512, 8, 640, 128], P('req', 'kv'), may hold values from -6 to 6
- cache_lengths: int32 [512], P('req'), may hold values from 1 to 640, as said below
- positions: int32 [512], P('req'), may hold values from 640 to 16383
- output_weight: bfloat16 [4096, 4096], P(None, 'req'), may hold values from -0.09375 to 0.09375
- mlp_gain: float32 [4096], P('req'), may hold values from 0.1 to 1.9
- gate_weight: bfloat16 [4096, 14336], P('req', 'kv'), may hold values from -0.09375 to 0.09375
- up_weight: bfloat16 [4096, 14336], P('req', 'kv'), may hold values from -0.09375 to 0.09375
- down_weight: bfloat16 [14336, 4096], P('kv', 'req'), may hold values from -0.046875 to 0.046875
Outputs:
- output: bfloat16 [512, 4096], P('kv', 'req')
Inputs may be any that keep to these rules, and one draw needn't show every extreme that they name: `cache_lengths`: each request's filled slots; some request has exactly 640 and some exactly 1.
All inputs are finite; a program needn't handle non-finite values.
Results may differ from a plain program's by a relative error of at most 0.025.
Values may be sent and summed in bfloat16 or wider, within the bound.
A program may use at most 128 MiB of HBM per device.

v0:
```python
import math

import jax
import jax.numpy as jnp
from jax import lax
from jax.sharding import PartitionSpec as P

MODEL_WIDTH = 4096
WINDOW = 512
SINKS = 4


EPS = 1e-05
THETA = 10000.0


def apply_rotary(vectors, places):
    half = vectors.shape[-1] // 2
    freqs = jnp.exp(
        jnp.arange(half, dtype=jnp.float32) * (-2.0 * math.log(THETA) / vectors.shape[-1])
    )
    angles = places.astype(jnp.float32)[:, None] * freqs[None, :]
    cosine = jnp.cos(angles)[:, None, :]
    sine = jnp.sin(angles)[:, None, :]
    first = vectors[..., :half]
    second = vectors[..., half:]
    return jnp.concatenate(
        [first * cosine - second * sine, second * cosine + first * sine], axis=-1
    )


def attend(query_rows, keys, values, new_key, new_value, allowed):
    factor = 1.0 / math.sqrt(query_rows.shape[-1])
    scores = (
        jnp.einsum("bgd,bjd->bgj", query_rows, keys, preferred_element_type=jnp.float32) * factor
    )
    scores = jnp.where(allowed[:, None, :], scores, -1e30)
    own = jnp.einsum("bgd,bd->bg", query_rows, new_key, preferred_element_type=jnp.float32) * factor
    peak = jnp.maximum(jnp.max(scores, axis=-1), own)
    expo = jnp.where(allowed[:, None, :], jnp.exp(scores - peak[..., None]), 0.0)
    own_expo = jnp.exp(own - peak)
    denom = jnp.sum(expo, axis=-1) + own_expo
    weights = (expo / denom[..., None]).astype(jnp.bfloat16)
    own_weight = (own_expo / denom).astype(jnp.bfloat16)
    mixed = jnp.einsum("bgj,bjd->bgd", weights, values, preferred_element_type=jnp.float32)
    mixed = (
        mixed
        + own_weight.astype(jnp.float32)[..., None] * new_value.astype(jnp.float32)[:, None, :]
    )
    return mixed.astype(jnp.bfloat16)


def shards(
    residual_in,
    attn_gain,
    query_weight,
    key_matrix,
    value_matrix,
    key_cache,
    cached_values,
    cache_lengths,
    positions,
    output_weight,
    mlp_gain,
    gate_weight,
    up_weight,
    down_weight,
):
    tokens = lax.all_to_all(residual_in, "req", split_axis=0, concat_axis=1, tiled=True)
    local_rows = tokens.shape[0]
    heads_here = key_cache.shape[1]
    head_size = key_cache.shape[3]
    query_group = query_weight.shape[1] // (heads_here * head_size)
    stream = tokens.astype(jnp.float32)
    normed_input = (
        stream
        / jnp.sqrt(jnp.sum(stream * stream, axis=-1, keepdims=True) / MODEL_WIDTH + EPS)
        * attn_gain
    ).astype(jnp.bfloat16)
    query_rows = jnp.dot(normed_input, query_weight, preferred_element_type=jnp.float32).reshape(
        local_rows, heads_here * query_group, head_size
    )
    query_rows = (
        apply_rotary(query_rows, positions)
        .astype(jnp.bfloat16)
        .reshape(local_rows, heads_here, query_group, head_size)
    )
    fresh_keys = jnp.dot(normed_input, key_matrix, preferred_element_type=jnp.float32).reshape(
        local_rows, heads_here, head_size
    )
    fresh_keys = apply_rotary(fresh_keys, positions).astype(jnp.bfloat16)
    fresh_values = (
        jnp.dot(normed_input, value_matrix, preferred_element_type=jnp.float32)
        .reshape(local_rows, heads_here, head_size)
        .astype(jnp.bfloat16)
    )
    slots = jnp.arange(key_cache.shape[2], dtype=jnp.int32)[None, :]
    limit = cache_lengths[:, None]
    allowed = (slots < limit) & ((slots < SINKS) | (slots > limit - WINDOW))
    results = [
        attend(
            query_rows[:, 0],
            key_cache[:, 0],
            cached_values[:, 0],
            fresh_keys[:, 0],
            fresh_values[:, 0],
            allowed,
        )
    ]
    attended_rows = jnp.stack(results, axis=1).reshape(
        local_rows, heads_here * query_group * head_size
    )
    features = attended_rows.shape[1]
    kv_place = lax.axis_index("kv")
    weight_rows = lax.dynamic_slice_in_dim(output_weight, kv_place * features, features, 0)
    partial_mix = jnp.dot(
        lax.all_gather(attended_rows, "req", axis=0, tiled=True),
        weight_rows,
        preferred_element_type=jnp.float32,
    )
    mixed = lax.psum(partial_mix.astype(jnp.bfloat16), "kv").astype(jnp.float32)
    middle = residual_in.astype(jnp.float32) + mixed
    scaled = (middle * mlp_gain).astype(jnp.bfloat16)
    squares = jnp.sum(middle * middle, axis=-1)
    gate_part = jnp.dot(scaled, gate_weight, preferred_element_type=jnp.float32)
    upper_part = jnp.dot(scaled, up_weight, preferred_element_type=jnp.float32)
    gate_total, upper_total, square_total = (
        lax.psum(gate_part.astype(jnp.bfloat16), "req").astype(jnp.float32),
        lax.psum(upper_part.astype(jnp.bfloat16), "req").astype(jnp.float32),
        lax.psum(squares.astype(jnp.bfloat16), "req").astype(jnp.float32),
    )
    inverse = (1.0 / jnp.sqrt(square_total / MODEL_WIDTH + EPS))[:, None]
    hidden = (jax.nn.silu(gate_total * inverse) * (upper_total * inverse)).astype(jnp.bfloat16)
    partial_out = jnp.dot(hidden, down_weight, preferred_element_type=jnp.float32)
    summed = lax.psum_scatter(
        partial_out.astype(jnp.bfloat16), "kv", scatter_dimension=0, tiled=True
    ).astype(jnp.float32)
    share = summed.shape[0]
    base_rows = lax.dynamic_slice_in_dim(middle, kv_place * share, share, 0)
    return (base_rows + summed).astype(jnp.bfloat16)


def solution(mesh):
    return jax.shard_map(
        shards,
        mesh=mesh,
        in_specs=(
            P(None, "req"),
            P(),
            P(None, "kv"),
            P(None, "kv"),
            P(None, "kv"),
            P("req", "kv", None, None),
            P("req", "kv", None, None),
            P("req"),
            P("req"),
            P(None, "req"),
            P("req"),
            P("req", "kv"),
            P("req", "kv"),
            P("kv", "req"),
        ),
        out_specs=P("kv", "req"),
        check_vma=False,
    )
```

profile of v0, /device:TPU:0, one launch (start us, length us, event | category | flops | bytes accessed | tf_op | source)
XLA Modules:
  0.0 266.5 jit_solution(15984500769440598371)
XLA Ops:
  6.5 0.0 copy-start
  6.5 8.1 %all-to-all-start = ((bf16[16,32,256]{2,1,0:T(8,128)(2,1)}), bf16[16,32,256]{2,1,0:T(8,128)(2,1)S(1)}, u32[]{:S(2)}, u32[]{:S(2)}) async-start(bf16[16,32,256]{2,1,0:T(8,128)(2,1)} %bitcast.48), calls=%async_computation | async-start | bytes 524288 | tf_op jit(solution)/shard_map/all_to_all | solution.py:69
  14.6 0.0 all-reduce.4.cloned.1.call-start
  14.7 0.7 broadcast_add_fusion
  15.4 0.7 fusion.29
  16.1 0.7 mul.176
  16.9 0.0 copy-start.10
  16.9 6.4 %copy.30 = bf16[512,4096]{1,0:T(8,128)(2,1)} copy(bf16[512,4096]{0,1:T(8,128)(2,1)} %bitcast.49) | data formatting | bytes 8388608 | tf_op jit(solution)/shard_map/dot_general | solution.py:80
  23.3 0.0 copy-done.10
  23.3 0.0 copy-start.7
  23.3 0.1 multiply_cosine_fusion.1
  23.5 0.0 all-to-all-done
  23.5 0.2 fusion.19
  23.7 0.1 fusion.22
  23.8 0.2 copy.24
  24.0 0.1 reshape.203
  24.1 0.0 copy-start.1
  24.2 0.0 copy-done.7
  24.2 0.0 copy-start.2
  24.2 1.7 convolution_bitcast_fusion
  25.9 0.1 fusion.45
  26.1 0.5 copy-done.1
  26.6 1.3 fusion.51
  27.9 0.0 copy-start.9
  28.0 0.1 subtract_convert_fusion
  28.1 0.1 pad_maximum_fusion
  28.1 0.1 maximum_bitcast_fusion
  28.2 0.1 fusion.31
  28.4 0.0 copy-done.2
  28.4 1.8 fusion.50
  30.2 0.3 fusion.24
  30.6 0.0 copy-done.9
  30.6 0.3 fusion.18
  30.9 0.0 copy-start.3
  30.9 0.0 copy-start.5
  30.9 0.0 copy-start.8
  30.9 3.6 %fusion.12 = bf16[32,4,128]{2,1,0:T(4,128)(2,1)S(1)} fusion(bf16[32,1,640,128]{3,2,1,0:T(8,128)(2,1)} %param.20, f32[32,4,640]{2,1,0:T(4,128)S(1)} %get-tuple-element.18, f32[32,4]{1,0:T(8,128)S(1)} %get-tuple-element.12, f32[32,4]{1,0:T(8,128)S(1)} %multiply_maximum_fusion, pred[32,640]{1,0:T(8,128)(4,1)S(1)} %fusion.29, f32[32,128]{1,0:T(8,128)S(1)} %fusion.18, ...), kind=kOutput, calls=%fused_computation.12 | convolution fusion | flops 21348352 | bytes 5641728 | tf_op jit(solution)/shard_map/bgj,bjd->bgd/dot_general | solution.py:45
  34.5 24.4 %all_gather.3 = bf16[512,512]{1,0:T(8,128)(2,1)S(1)} all-gather(bf16[32,512]{1,0:T(8,128)(2,1)S(1)} %bitcast.52), channel_id=1, replica_groups=mesh['req'=16,'kv'=8] {'req'}, dimensions={0}, use_global_device_ids=true | all-gather | bytes 557056 | tf_op jit(solution)/shard_map/all_gather | solution.py:117
  58.9 0.0 copy-done
  58.9 1.0 convolution_convert_fusion.2
  59.9 0.0 all-reduce.4.cloned.1.call-update
  60.0 0.0 all-reduce.6.cloned.1.call-start
  60.0 59.4 %all-reduce.4.cloned.1.call-done = bf16[512,256]{1,0:T(8,128)(2,1)} async-done(((bf16[512,256]{1,0:T(8,128)(2,1)}), bf16[512,256]{1,0:T(8,128)(2,1)}) %all-reduce.4.cloned.1.call-update) | async-done | bytes 262160 | tf_op jit(solution)/shard_map/psum | solution.py:121
  119.4 0.0 copy-done.3
  119.4 0.0 copy-done.5
  119.4 0.0 copy-done.8
  119.4 0.0 copy-start.6
  119.4 2.9 %convolution_convert_fusion = bf16[512,1792]{1,0:T(8,128)(2,1)} fusion(bf16[256,1792]{1,0:T(8,128)(2,1)S(1)} %copy-done.5, f32[256]{0:T(256)S(1)} %copy-done.8, bf16[512,256]{1,0:T(8,128)(2,1)} %all-reduce.4.cloned.1.call-done, bf16[512,256]{1,0:T(8,128)(2,1)S(1)} %copy-done.3), kind=kOutput, calls=%fused_computation.5 | convolution fusion | flops 471334912 | bytes 3277824 | tf_op jit(solution)/shard_map/dot_general | solution.py:126
  122.4 0.0 copy-done.6
  122.4 0.0 copy-start.4
  122.4 2.9 %convolution_convert_fusion.1 = bf16[512,1792]{1,0:T(8,128)(2,1)} fusion(bf16[256,1792]{1,0:T(8,128)(2,1)S(1)} %copy-done.6, f32[256]{0:T(256)S(1)} %copy-done.8, bf16[512,256]{1,0:T(8,128)(2,1)} %all-reduce.4.cloned.1.call-done, bf16[512,256]{1,0:T(8,128)(2,1)S(1)} %copy-done.3), kind=kOutput, calls=%fused_computation.6 | convolution fusion | flops 471334912 | bytes 3277824 | tf_op jit(solution)/shard_map/dot_general | solution.py:125
  125.3 0.0 all-reduce.6.cloned.1.call-update
  125.3 0.0 reduce-scatter.2.cloned.1.call-start
  125.4 0.0 copy-done.4
  125.4 0.2 convert_add_fusion
  125.5 41.1 %psum.30 = bf16[512]{0:T(512)(128)(2,1)S(1)} all-reduce(bf16[512]{0:T(512)(128)(2,1)S(1)} %get-tuple-element.8), channel_id=1, replica_groups=mesh['req'=16,'kv'=8] {'req'}, use_global_device_ids=true, to_apply=%region_6.7 | all-reduce | flops 512 | bytes 2048 | tf_op jit(solution)/shard_map/psum | solution.py:130
  166.7 57.5 %all-reduce.6.cloned.1.call-done = (bf16[512,1792]{1,0:T(8,128)(2,1)}, bf16[512,1792]{1,0:T(8,128)(2,1)}) async-done(((bf16[512,1792]{1,0:T(8,128)(2,1)}, bf16[512,1792]{1,0:T(8,128)(2,1)}), (bf16[512,1792]{1,0:T(8,128)(2,1)}, bf16[512,1792]{1,0:T(8,128)(2,1)})) %all-reduce.6.cloned.1.call-update) | async-done | bytes 3670032 | tf_op jit(solution)/shard_map/psum | solution.py:129
  224.2 4.4 %fusion.5 = bf16[512,256]{1,0:T(8,128)(2,1)} fusion(bf16[1792,256]{1,0:T(8,128)(2,1)} %param.27, bf16[512,1792]{1,0:T(8,128)(2,1)} %get-tuple-element.5, bf16[512,1792]{1,0:T(8,128)(2,1)} %get-tuple-element.6, f32[512]{0:T(512)S(1)} %add_rsqrt_fusion), kind=kOutput, calls=%fused_computation.9 | convolution fusion | flops 479068160 | bytes 4851712 | tf_op jit(solution)/shard_map/dot_general | solution.py:134
  228.6 0.0 reduce-scatter.2.cloned.1.call-update
  228.6 30.0 %reduce-scatter.2.cloned.1.call-done = bf16[64,256]{1,0:T(8,128)(2,1)} async-done(((bf16[512,256]{1,0:T(8,128)(2,1)}), bf16[64,256]{1,0:T(8,128)(2,1)}) %reduce-scatter.2.cloned.1.call-update) | async-done | bytes 32784 | tf_op jit(solution)/shard_map/reduce_scatter | solution.py:135
  258.6 1.4 add_convert_fusion
  (10 shorter events, 0.2 us)
Async XLA Ops:
  6.5 52.4 %copy-start = (bf16[4096,256]{1,0:T(8,128)(2,1)S(1)}, bf16[4096,256]{1,0:T(8,128)(2,1)}, u32[]{:S(2)}) copy-start(bf16[4096,256]{1,0:T(8,128)(2,1)} %param.23) | copy-start | bytes 6291460
  6.5 16.9 %all-to-all-start = ((bf16[16,32,256]{2,1,0:T(8,128)(2,1)}), bf16[16,32,256]{2,1,0:T(8,128)(2,1)S(1)}, u32[]{:S(2)}, u32[]{:S(2)}) async-start(bf16[16,32,256]{2,1,0:T(8,128)(2,1)} %bitcast.48), calls=%async_computation | async-start | bytes 524288 | tf_op jit(solution)/shard_map/all_to_all | solution.py:69
  14.6 104.8 %all-reduce.4.cloned.1.call-start = ((), (), s32[]{:S(2)}) async-start(), calls=%async_computation.2 | async-start | bytes 524288 | tf_op jit(solution)/shard_map/psum | solution.py:121
  16.9 6.5 %copy-start.10 = (s32[32]{0:T(128)S(1)}, s32[32]{0:T(128)}, u32[]{:S(2)}) copy-start(s32[32]{0:T(128)} %param.22) | copy-start | bytes 388
  23.3 0.9 copy-start.7
  24.1 2.5 copy-start.1
  24.2 4.2 %copy-start.2 = (bf16[32,1,640,128]{3,2,1,0:T(8,128)(2,1)S(1)}, bf16[32,1,640,128]{3,2,1,0:T(8,128)(2,1)}, u32[]{:S(2)}) copy-start(bf16[32,1,640,128]{3,2,1,0:T(8,128)(2,1)} %param.19) | copy-start | bytes 15728644
  27.9 2.6 copy-start.9
  30.9 88.5 %copy-start.3 = (bf16[512,256]{1,0:T(8,128)(2,1)S(1)}, bf16[512,256]{1,0:T(8,128)(2,1)}, u32[]{:S(2)}) copy-start(bf16[512,256]{1,0:T(8,128)(2,1)} %param.14) | copy-start | bytes 786436
  30.9 88.5 %copy-start.5 = (bf16[256,1792]{1,0:T(8,128)(2,1)S(1)}, bf16[256,1792]{1,0:T(8,128)(2,1)}, u32[]{:S(2)}) copy-start(bf16[256,1792]{1,0:T(8,128)(2,1)} %param.26) | copy-start | bytes 2752516
  30.9 88.5 %copy-start.8 = (f32[256]{0:T(256)S(1)}, f32[256]{0:T(256)}, u32[]{:S(2)}) copy-start(f32[256]{0:T(256)} %param.24) | copy-start | bytes 3076
  60.0 164.2 %all-reduce.6.cloned.1.call-start = ((), (), s32[]{:S(2)}) async-start(), calls=%async_computation.4 | async-start | bytes 7340032 | tf_op jit(solution)/shard_map/psum | solution.py:129
  119.4 3.0 %copy-start.6 = (bf16[256,1792]{1,0:T(8,128)(2,1)S(1)}, bf16[256,1792]{1,0:T(8,128)(2,1)}, u32[]{:S(2)}) copy-start(bf16[256,1792]{1,0:T(8,128)(2,1)} %param.25) | copy-start | bytes 2752516
  122.4 3.0 %copy-start.4 = (bf16[512,256]{1,0:T(8,128)(2,1)S(1)}, bf16[512,256]{1,0:T(8,128)(2,1)}, u32[]{:S(2)}) copy-start(bf16[512,256]{1,0:T(8,128)(2,1)} %all-reduce.4.cloned.1.call-done) | copy-start | bytes 786436
  125.3 133.3 %reduce-scatter.2.cloned.1.call-start = ((), (), s32[]{:S(2)}) async-start(), calls=%async_computation.3 | async-start | bytes 294912 | tf_op jit(solution)/shard_map/reduce_scatter | solution.py:135
Sparse Core Ops, SparseCore 0:
  60.1 59.2 all-reduce.3
  125.4 98.6 all-reduce.5
  228.8 29.7 reduce-scatter.1
where the time goes:
time: 267 us; the launch traced here: 266 us
  waiting for transfers between devices  147 us (55%)
  blocking collectives  65.5 us (25%)
  matrix products  20.2 us (8%)
  between operations  13.4 us (5%)
  starting transfers between devices  8.22 us (3%)
  local copies, waits for them, and re-layouts  8.06 us (3%)
  other arithmetic  4.23 us (2%)
    psum x1, waiting for transfers between devices, shards(): mixed = lax.psum(partial_mix.astype(jnp.bfloat16), 'kv').astype(jnp.float32)  59.4 us
    psum x1, waiting for transfers between devices, shards(): lax.psum(upper_part.astype(jnp.bfloat16), 'req').astype(jnp.float32)  57.5 us
    psum x1, blocking collectives, shards(): lax.psum(squares.astype(jnp.bfloat16), 'req').astype(jnp.float32)  41.1 us
    reduce_scatter x1, waiting for transfers between devices, shards(): lax.psum_scatter(partial_out.astype(jnp.bfloat16), 'kv', scatter_dimensio...  30 us
    all_gather x1, blocking collectives, shards(): lax.all_gather(attended_rows, 'req', axis=0, tiled=True)  24.4 us
    all_to_all x1, starting transfers between devices, shards(): lax.all_to_all(residual_in, 'req', split_axis=0, concat_axis=1, tiled=True)  8.09 us
    dot_general x1, local copies, waits for them, and re-layouts, shards(): jnp.dot(normed_input, query_weight, preferred_element_type=jnp.float32)  6.45 us
  transfers between devices with their start and end apart: 4, of which 3 were waited for; matrix products, arithmetic and copies ran while one was open for 3% of the time, Pallas kernels for 0%

commit v1 on v0

v1 whole, which is shorter than its diff:
```python
import functools
import math

import jax
import jax.numpy as jnp
from jax import lax
from jax.experimental import pallas as pl
from jax.experimental.pallas import tpu as pltpu
from jax.sharding import PartitionSpec as P

MODEL_WIDTH = 4096
WINDOW = 512
SINKS = 4
EPS = 1e-05
THETA = 10000.0

NR = 16
NK = 8
ROWS = 32
COLS = 256
FFK = 1792
HEADS = 4
HD = 128
SLOTS = 640
CHUNK = 896

BF = jnp.bfloat16
F32 = jnp.float32
MESH = pl.DeviceIdType.MESH
NT = (((1,), (1,)), ((), ()))
TN = (((0,), (0,)), ((), ()))


def dot(a, b):
    return jnp.dot(a, b, preferred_element_type=F32)


def piece_offset(l):
    return 448 * l + 64 * (l % 2)


def kernel(
    lens, resid, gain1, wq, wk, wv, kc, vc, cosf, sinf, wo, gain2, gw, uw, dw,
    out,
    tok, nrm, wq_v, wk_v, wv_v, k_v, v_v, q3, k3, v3, o3, att, attb, wo_v, res_v,
    gp, up, pk, wp, al, mid, pb, rh, rf, acc1, acc3, hb, dw_v, fs, fb, ownf, sqa, sql, sqm,
    ld, tokS, tokR, wS, wR, attS, attR, b2, yS, alR, lS, al2S, al2R, sqS, sqR, sqlS, sqlR, sqmS, sqmR,
    rhS, rhR, rfS, rfR, hmS, hR, hlS, h2S, h2R, fS, fR,
):
    r = lax.axis_index("req")
    k = lax.axis_index("kv")
    x, z = r // 4, r % 4
    c = k % 2
    l = (1 - c) * x + c * z
    m = (1 - c) * z + c * x

    def dev(li, mi):
        return ((1 - c) * (4 * li + mi) + c * (4 * mi + li), k)

    def rc(src, dst, ss, rs, to):
        return pltpu.make_async_remote_copy(
            src_ref=src, dst_ref=dst, send_sem=ss, recv_sem=rs, device_id=to, device_id_type=MESH
        )

    def arrived(ref, sem):
        pltpu.make_async_copy(ref, ref, sem).wait()

    barrier = pltpu.get_barrier_semaphore()
    for d in range(1, NR):
        pl.semaphore_signal(barrier, inc=1, device_id=((r + d) % NR, k), device_id_type=MESH)
    for d in range(1, NK):
        pl.semaphore_signal(barrier, inc=1, device_id=(r, (k + d) % NK), device_id_type=MESH)

    loads = {}

    def load(name, index, src, dst):
        loads[name] = pltpu.make_async_copy(src, dst, ld.at[index])
        loads[name].start()

    own_tok = pltpu.make_async_copy(resid.at[pl.ds(ROWS * r, ROWS), :], tok.at[r], tokR.at[r])
    own_tok.start()
    load("g3", 0, gw.at[:, pl.ds(384, 128)], gp.at[0])
    load("g10", 1, gw.at[:, pl.ds(1280, 128)], gp.at[1])
    load("u3", 2, uw.at[:, pl.ds(384, 128)], up.at[0])
    load("u10", 3, uw.at[:, pl.ds(1280, 128)], up.at[1])
    load("wq", 4, wq, wq_v)
    load("wk", 5, wk, wk_v)
    load("wv", 6, wv, wv_v)
    load("kc", 7, kc, k_v)
    load("vc", 8, vc, v_v)
    load("wo", 9, wo, wo_v)
    load("res", 10, resid.at[pl.ds(64 * k, 64), :], res_v)
    load("dw", 11, dw, dw_v)

    pl.semaphore_wait(barrier, NR - 1 + NK - 1)
    for d in range(1, NK):
        pl.semaphore_signal(b2, inc=1, device_id=(r, (k + d) % NK), device_id_type=MESH)

    def tok_copy(d):
        to = (r + d) % NR
        return rc(resid.at[pl.ds(ROWS * to, ROWS), :], tok.at[r], tokS.at[d - 1], tokR.at[r], (to, k))

    @pl.loop(1, NR)
    def _(d):
        tok_copy(d).start()

    def w_copies(d):
        to = (l + d) % 4
        off = pl.multiple_of(piece_offset(to), 128)
        pieces = (
            (gw.at[:, pl.ds(off, 384)], wp.at[l, :, pl.ds(0, 384)]),
            (uw.at[:, pl.ds(off, 384)], wp.at[l, :, pl.ds(384, 384)]),
            (pk.at[to], wp.at[l, :, pl.ds(768, 128)]),
        )
        if d == 0:
            return [pltpu.make_async_copy(s, t, wR.at[l]) for s, t in pieces]
        return [rc(s, t, wS.at[3 * (d - 1) + i], wR.at[l], dev(to, m)) for i, (s, t) in enumerate(pieces)]

    w_sends = {d: w_copies(d) for d in range(4)}
    for d in (1, 3, 2, 0):
        w_sends[d][0].start()
        w_sends[d][1].start()
    for name in ("g3", "g10", "u3", "u10"):
        loads[name].wait()
    low = lax.broadcasted_iota(jnp.int32, (COLS, 128), 1) < 64
    for t in range(2):
        g = gp[t].astype(F32)
        u = pltpu.roll(up[t].astype(F32), 64, 1)
        pk[2 * t] = jnp.where(low, g, u).astype(BF)
        pk[2 * t + 1] = jnp.where(low, u, g).astype(BF)
    for d in (1, 3, 2, 0):
        w_sends[d][2].start()

    q3[...] = jnp.zeros_like(q3)
    k3[...] = jnp.zeros_like(k3)
    v3[...] = jnp.zeros_like(v3)

    squares = jnp.zeros((ROWS, COLS), F32)
    for i in range(NR):
        arrived(tok.at[i], tokR.at[i])
    for i in range(NR):
        t = tok[i].astype(F32)
        squares = squares + t * t
    scale = 1.0 / jnp.sqrt(jnp.sum(squares, axis=-1, keepdims=True) / MODEL_WIDTH + EPS)
    for i in range(NR):
        nrm[i] = (tok[i].astype(F32) * scale * gain1[:, COLS * i : COLS * (i + 1)]).astype(BF)
    loads["wq"].wait()
    loads["wk"].wait()
    loads["wv"].wait()
    q = jnp.zeros((ROWS, HEADS * HD), F32)
    kn = jnp.zeros((ROWS, HD), F32)
    vn = jnp.zeros((ROWS, HD), F32)
    for i in range(NR):
        n = nrm[i]
        q = q + dot(n, wq_v[COLS * i : COLS * (i + 1), :])
        kn = kn + dot(n, wk_v[COLS * i : COLS * (i + 1), :])
        vn = vn + dot(n, wv_v[COLS * i : COLS * (i + 1), :])
    cs, sn = cosf[...], sinf[...]

    def rotate(v):
        return (v * cs + pltpu.roll(v, 64, 1) * sn).astype(BF).astype(F32)

    kn = rotate(kn)
    vn = vn.astype(BF).astype(F32)
    for h in range(HEADS):
        q3[pl.ds(h, ROWS, stride=8), :] = rotate(q[:, HD * h : HD * (h + 1)])
        k3[pl.ds(h, ROWS, stride=8), :] = kn
        v3[pl.ds(h, ROWS, stride=8), :] = vn

    loads["kc"].wait()
    loads["vc"].wait()
    factor = 1.0 / math.sqrt(HD)
    slot = lax.broadcasted_iota(jnp.int32, (8, SLOTS), 1)

    def attend(b):
        rows = pl.ds(pl.multiple_of(8 * b, 8), 8)
        qb = q3[rows, :]
        s = lax.dot_general(qb.astype(BF), k_v[b], NT, preferred_element_type=F32) * factor
        n = lens[b]
        ok = (slot < n) & ((slot < SINKS) | (slot > n - WINDOW))
        s = jnp.where(ok, s, -1e30)
        own = jnp.sum(qb * k3[rows, :], axis=-1, keepdims=True) * factor
        peak = jnp.maximum(jnp.max(s, axis=-1, keepdims=True), own)
        e = jnp.where(ok, jnp.exp(s - peak), 0.0)
        eo = jnp.exp(own - peak)
        inv = 1.0 / (jnp.sum(e, axis=-1, keepdims=True) + eo)
        w = (e * inv).astype(BF)
        wo_ = (eo * inv).astype(BF).astype(F32)
        o3[rows, :] = dot(w, v_v[b]) + wo_ * v3[rows, :]

    kd = r // 2

    def att_copy(half, d):
        to = (r + d) % NR
        rows = pl.ds(16 * half, 16)
        there = pl.ds(pl.multiple_of((r % 2) * 32 + 16 * half, 16), 16)
        return (att.at[rows, :], attb.at[k, there, :], attS.at[16 * half + d], attR.at[k, r % 2], (to, kd))

    for half in range(2):

        @pl.loop(0, 4)
        def _(g):
            for j in range(4):
                attend(16 * half + 4 * g + j)

        for h in range(HEADS):
            att[16 * half : 16 * half + 16, HD * h : HD * (h + 1)] = o3[
                pl.ds(128 * half + h, 16, stride=8), :
            ].astype(BF)
        if half == 0:
            pl.semaphore_wait(b2, NK - 1)

        @pl.when(k == kd)
        def _():
            src, dst, _, rs, _ = att_copy(half, 0)
            pltpu.make_async_copy(src, dst, rs).start()

        @pl.when(k != kd)
        def _():
            rc(*att_copy(half, 0)).start()

        @pl.loop(1, NR)
        def _(d):
            rc(*att_copy(half, d)).start()

    loads["wo"].wait()
    loads["res"].wait()
    for i in range(NK):
        for p in range(2):
            arrived(attb.at[i, pl.ds(32 * p, 32), :], attR.at[i, p])
    o = res_v[...].astype(F32)
    for i in range(NK):
        o = o + dot(attb[i], wo_v[512 * i : 512 * (i + 1), :])
    mid[...] = o
    blk = pl.ds(pl.multiple_of(64 * k, 64), 64)
    al[l, blk, :] = (o * gain2[...]).astype(BF)
    o2 = jnp.concatenate([o * o, jnp.zeros_like(o)], axis=0)
    sqa[k] = lax.dot_general(
        jnp.ones((8, COLS), F32), o2, NT, preferred_element_type=F32, precision=lax.Precision.HIGHEST
    )

    ends = []

    def go(copy):
        copy.start()
        ends.append(copy)

    order = (1, 7, 2, 6, 3, 5, 4)
    for i, d in enumerate(order):
        kp = (k + d) % NK
        cp = kp % 2
        lp = (1 - cp) * x + cp * z
        go(rc(al.at[l, blk, :], al.at[lp, blk, :], yS.at[i], alR.at[lp, k], (r, kp)))
        go(rc(sqa.at[k], sqa.at[k], sqS.at[i], sqR.at[k], (r, kp)))
    nxt, prv = (l + 1) % 4, (l + 3) % 4
    for i, d in enumerate((0,) + order):
        kp = (k + d) % NK
        at = pl.ds(pl.multiple_of(64 * kp, 64), 64)
        if d:
            arrived(al.at[l, at, :], alR.at[l, kp])
        go(rc(al.at[l, at, :], al.at[l, at, :], lS.at[0, i], alR.at[l, kp], dev(nxt, m)))
        go(rc(al.at[l, at, :], al.at[l, at, :], lS.at[1, i], alR.at[l, kp], dev(prv, m)))
    for d in order:
        kp = (k + d) % NK
        arrived(sqa.at[kp], sqR.at[kp])
    sub = lax.broadcasted_iota(jnp.int32, (8, 128), 0)
    t = jnp.zeros((8, 128), F32)
    for i in range(NK):
        t = t + jnp.where(sub == i, sqa[i], 0.0)
    sql[l] = t
    for d in range(1, 4):
        go(rc(sql.at[l], sql.at[l], sqlS.at[d - 1], sqlR.at[l], dev((l + d) % 4, m)))
    for i, d in enumerate((0,) + order):
        kp = (k + d) % NK
        at = pl.ds(pl.multiple_of(64 * kp, 64), 64)
        first = pl.ds(pl.multiple_of(64 * kp, 32), 32)
        second = pl.ds(pl.multiple_of(64 * kp + 32, 32), 32)
        arrived(al.at[prv, at, :], alR.at[prv, kp])
        go(rc(al.at[prv, first, :], al.at[prv, first, :], al2S.at[0, i], al2R.at[0, kp], dev(nxt, m)))
        arrived(al.at[nxt, at, :], alR.at[nxt, kp])
        go(rc(al.at[nxt, second, :], al.at[nxt, second, :], al2S.at[1, i], al2R.at[1, kp], dev(prv, m)))
    for d in range(1, 4):
        at = (l + d) % 4
        arrived(sql.at[at], sqlR.at[at])
    sqm[m] = sql[0] + sql[1] + sql[2] + sql[3]
    for d in range(1, 4):
        go(rc(sqm.at[m], sqm.at[m], sqmS.at[d - 1], sqmR.at[m], dev(l, (m + d) % 4)))
    far = (l + 2) % 4
    for i, d in enumerate((0,) + order):
        kp = (k + d) % NK
        arrived(al.at[far, pl.ds(pl.multiple_of(64 * kp, 32), 32), :], al2R.at[0, kp])
        arrived(al.at[far, pl.ds(pl.multiple_of(64 * kp + 32, 32), 32), :], al2R.at[1, kp])
    for i in range(4):
        arrived(wp.at[i], wR.at[i])

    def part(mi):
        rows = pl.ds(pl.multiple_of(128 * mi, 128), 128)
        total = dot(al[0, rows, :], wp[0])
        for i in range(1, 4):
            total = total + dot(al[i, rows, :], wp[i])
        return total

    m1, m2, m3 = (m + 1) % 4, (m + 2) % 4, (m + 3) % 4
    pb[2] = part(m2).astype(BF)
    go(rc(pb.at[2, pl.ds(0, 64), :], rh.at[0], rhS.at[0], rhR.at[0], dev(l, m1)))
    go(rc(pb.at[2, pl.ds(64, 64), :], rh.at[1], rhS.at[1], rhR.at[1], dev(l, m3)))
    acc1[...] = part(m1)
    acc3[...] = part(m3)
    arrived(rh.at[0], rhR.at[0])
    pb[0, 0:64, :] = (acc1[0:64, :] + rh[0].astype(F32)).astype(BF)
    pb[0, 64:128, :] = acc1[64:128, :].astype(BF)
    go(rc(pb.at[0], rf.at[0], rfS.at[0], rfR.at[0], dev(l, m1)))
    arrived(rh.at[1], rhR.at[1])
    pb[1, 0:64, :] = acc3[0:64, :].astype(BF)
    pb[1, 64:128, :] = (acc3[64:128, :] + rh[1].astype(F32)).astype(BF)
    go(rc(pb.at[1], rf.at[1], rfS.at[1], rfR.at[1], dev(l, m3)))
    acc1[...] = part(m)
    for d in range(1, 4):
        at = (m + d) % 4
        arrived(sqm.at[at], sqmR.at[at])
    sq = sqm[0] + sqm[1] + sqm[2] + sqm[3]
    pick = [
        lax.dot_general(
            sq,
            (sub == 2 * m + i).astype(F32),
            TN,
            preferred_element_type=F32,
            precision=lax.Precision.HIGHEST,
        )[0:64, :]
        for i in range(2)
    ]
    inv = 1.0 / jnp.sqrt(jnp.concatenate(pick, axis=0) / MODEL_WIDTH + EPS)
    arrived(rf.at[0], rfR.at[0])
    arrived(rf.at[1], rfR.at[1])
    mine = pl.ds(pl.multiple_of(128 * m, 128), 128)

    def tile(i):
        at = slice(128 * i, 128 * (i + 1))
        return (acc1[:, at] + rf[0, :, at].astype(F32) + rf[1, :, at].astype(F32)) * inv

    def silu(v):
        return v / (1.0 + jnp.exp(-v))

    for i in range(3):
        hb[l, mine, 128 * i : 128 * (i + 1)] = (silu(tile(i)) * tile(3 + i)).astype(BF)
    t = tile(6)
    lane = lax.broadcasted_iota(jnp.int32, (128, 128), 1)
    hb[l, mine, 384:512] = jnp.where(lane // 64 == l % 2, silu(t) * pltpu.roll(t, 64, 1), 0.0).astype(BF)

    for i, d in enumerate((1, 3, 2)):
        go(rc(hb.at[l, mine, :], hb.at[l, mine, :], hmS.at[i], hR.at[l, m], dev(l, (m + d) % 4)))
    for i, d in enumerate((0, 1, 3, 2)):
        mi = (m + d) % 4
        at = pl.ds(pl.multiple_of(128 * mi, 128), 128)
        if d:
            arrived(hb.at[l, at, :], hR.at[l, mi])
        go(rc(hb.at[l, at, :], hb.at[l, at, :], hlS.at[0, i], hR.at[l, mi], dev(nxt, m)))
        go(rc(hb.at[l, at, :], hb.at[l, at, :], hlS.at[1, i], hR.at[l, mi], dev(prv, m)))
    for i, d in enumerate((0, 1, 3, 2)):
        mi = (m + d) % 4
        at = pl.ds(pl.multiple_of(128 * mi, 128), 128)
        first = pl.ds(pl.multiple_of(128 * mi, 64), 64)
        second = pl.ds(pl.multiple_of(128 * mi + 64, 64), 64)
        arrived(hb.at[prv, at, :], hR.at[prv, mi])
        go(rc(hb.at[prv, first, :], hb.at[prv, first, :], h2S.at[0, i], h2R.at[0, mi], dev(nxt, m)))
        arrived(hb.at[nxt, at, :], hR.at[nxt, mi])
        go(rc(hb.at[nxt, second, :], hb.at[nxt, second, :], h2S.at[1, i], h2R.at[1, mi], dev(prv, m)))

    loads["dw"].wait()

    def last_copy(kp):
        return rc(fs.at[kp], fb.at[k], fS.at[kp], fR.at[k], (r, kp))

    for d in (0, 1, 3, 2):
        mi = (m + d) % 4
        at = pl.ds(pl.multiple_of(128 * mi, 128), 128)
        arrived(hb.at[far, pl.ds(pl.multiple_of(128 * mi, 64), 64), :], h2R.at[0, mi])
        arrived(hb.at[far, pl.ds(pl.multiple_of(128 * mi + 64, 64), 64), :], h2R.at[1, mi])
        y = dot(hb[0, at, 0:384], dw_v[0:384, :])
        for i in range(1, 4):
            off = piece_offset(i)
            y = y + dot(hb[i, at, 0:384], dw_v[off : off + 384, :])
        for i in range(2):
            off = 384 + 896 * i
            y = y + dot(hb[2 * i, at, 384:512] + hb[2 * i + 1, at, 384:512], dw_v[off : off + 128, :])
        for i in range(2):
            kp = 2 * mi + i
            fs[kp] = y[64 * i : 64 * (i + 1), :].astype(BF)

            @pl.when(kp == k)
            def _():
                ownf[...] = y[64 * i : 64 * (i + 1), :]

            @pl.when(kp != k)
            def _():
                last_copy(kp).start()

    total = mid[...] + ownf[...]
    for d in range(1, NK):
        kp = (k + d) % NK
        arrived(fb.at[kp], fR.at[kp])
        total = total + fb[kp].astype(F32)
    out[...] = total.astype(BF)

    @pl.loop(1, NR)
    def _(d):
        tok_copy(d).wait_send()

    for d in range(1, 4):
        for copy in w_sends[d]:
            copy.wait_send()
    for half in range(2):

        @pl.when(k != kd)
        def _():
            rc(*att_copy(half, 0)).wait_send()

        @pl.loop(1, NR)
        def _(d):
            rc(*att_copy(half, d)).wait_send()

    for copy in ends:
        copy.wait_send()
    for d in range(1, NK):
        last_copy((k + d) % NK).wait_send()


def shards(
    residual_in,
    attn_gain,
    query_weight,
    key_matrix,
    value_matrix,
    key_cache,
    cached_values,
    cache_lengths,
    positions,
    output_weight,
    mlp_gain,
    gate_weight,
    up_weight,
    down_weight,
):
    half = HD // 2
    freqs = jnp.exp(jnp.arange(half, dtype=F32) * (-2.0 * math.log(THETA) / HD))
    angles = positions.astype(F32)[:, None] * freqs[None, :]
    cosine, sine = jnp.cos(angles), jnp.sin(angles)
    cosf = jnp.concatenate([cosine, cosine], axis=-1)
    sinf = jnp.concatenate([-sine, sine], axis=-1)
    hbm = pl.BlockSpec(memory_space=pltpu.MemorySpace.HBM)
    vmem = pl.BlockSpec(memory_space=pltpu.MemorySpace.VMEM)
    smem = pl.BlockSpec(memory_space=pltpu.MemorySpace.SMEM)
    V = pltpu.VMEM
    dma = lambda *shape: pltpu.SemaphoreType.DMA(shape)
    return pl.pallas_call(
        kernel,
        out_shape=jax.ShapeDtypeStruct((64, COLS), BF),
        in_specs=[smem, hbm, vmem, hbm, hbm, hbm, hbm, hbm, vmem, vmem, hbm, vmem, hbm, hbm, hbm],
        out_specs=vmem,
        scratch_shapes=[
            V((NR, ROWS, COLS), BF),
            V((NR, ROWS, COLS), BF),
            V((MODEL_WIDTH, HEADS * HD), BF),
            V((MODEL_WIDTH, HD), BF),
            V((MODEL_WIDTH, HD), BF),
            V((ROWS, SLOTS, HD), BF),
            V((ROWS, SLOTS, HD), BF),
            V((8 * ROWS, HD), F32),
            V((8 * ROWS, HD), F32),
            V((8 * ROWS, HD), F32),
            V((8 * ROWS, HD), F32),
            V((ROWS, HEADS * HD), BF),
            V((NK, 64, HEADS * HD), BF),
            V((MODEL_WIDTH, COLS), BF),
            V((64, COLS), BF),
            V((2, COLS, 128), BF),
            V((2, COLS, 128), BF),
            V((4, COLS, 128), BF),
            V((4, COLS, CHUNK), BF),
            V((4, 512, COLS), BF),
            V((64, COLS), F32),
            V((3, 128, CHUNK), BF),
            V((2, 64, CHUNK), BF),
            V((2, 128, CHUNK), BF),
            V((128, CHUNK), F32),
            V((128, CHUNK), F32),
            V((4, 512, 512), BF),
            V((FFK, COLS), BF),
            V((NK, 64, COLS), BF),
            V((NK, 64, COLS), BF),
            V((64, COLS), F32),
            V((NK, 8, 128), F32),
            V((4, 8, 128), F32),
            V((4, 8, 128), F32),
            dma(12),
            dma(NR - 1),
            dma(NR),
            dma(9),
            dma(4),
            dma(32),
            dma(NK, 2),
            pltpu.SemaphoreType.REGULAR,
            dma(NK - 1),
            dma(4, NK),
            dma(2, NK),
            dma(2, NK),
            dma(2, NK),
            dma(NK - 1),
            dma(NK),
            dma(3),
            dma(4),
            dma(3),
            dma(4),
            dma(2),
            dma(2),
            dma(2),
            dma(2),
            dma(3),
            dma(4, 4),
            dma(2, 4),
            dma(2, 4),
            dma(2, 4),
            dma(NK),
            dma(NK),
        ],
        compiler_params=pltpu.CompilerParams(
            collective_id=0, has_side_effects=True, vmem_limit_bytes=56 << 20
        ),
    )(
        cache_lengths,
        residual_in,
        attn_gain.reshape(1, MODEL_WIDTH),
        query_weight,
        key_matrix,
        value_matrix,
        key_cache.reshape(ROWS, SLOTS, HD),
        cached_values.reshape(ROWS, SLOTS, HD),
        cosf,
        sinf,
        output_weight,
        mlp_gain.reshape(1, COLS),
        gate_weight,
        up_weight,
        down_weight,
    )


def solution(mesh):
    return jax.shard_map(
        shards,
        mesh=mesh,
        in_specs=(
            P(None, "req"),
            P(),
            P(None, "kv"),
            P(None, "kv"),
            P(None, "kv"),
            P("req", "kv", None, None),
            P("req", "kv", None, None),
            P("req"),
            P("req"),
            P(None, "req"),
            P("req"),
            P("req", "kv"),
            P("req", "kv"),
            P("kv", "req"),
        ),
        out_specs=P("kv", "req"),
        check_vma=False,
    )
```

time: 267 us -> 88.6 us (0.33)
  waiting for transfers between devices: 147 us -> 0 us
  Pallas kernels: 0 us -> 84.4 us
  blocking collectives: 65.5 us -> 0 us
  matrix products: 20.2 us -> 0 us
  between operations: 13.4 us -> 0.02 us
  starting transfers between devices: 8.22 us -> 0 us
  local copies, waits for them, and re-layouts: 8.06 us -> 1.38 us
  other arithmetic: 4.23 us -> 1.5 us
    psum x2 -> x0, waiting for transfers between devices: 117 us -> none  [the longest x1 59.4 us: shards(): mixed = lax.psum(partial_mix.astype(jnp.bfloat16), 'kv').astype(jnp.float32)]
    pallas_call x0 -> x1, Pallas kernels: none -> 84.4 us  [shards(): pl.pallas_call(kernel, out_shape=jax.ShapeDtypeStruct((64, COLS), BF), in...]
    psum x1 -> x0, blocking collectives: 41.1 us -> none  [shards(): lax.psum(squares.astype(jnp.bfloat16), 'req').astype(jnp.float32)]
    reduce_scatter x1 -> x0, waiting for transfers between devices: 30 us -> none  [shards(): lax.psum_scatter(partial_out.astype(jnp.bfloat16), 'kv', scatter_dimensio...]
    all_gather x1 -> x0, blocking collectives: 24.4 us -> none  [shards(): lax.all_gather(attended_rows, 'req', axis=0, tiled=True)]
    dot_general x10 -> x0, matrix products: 20.2 us -> none  [the longest x1 4.43 us: shards(): jnp.dot(hidden, down_weight, preferred_element_type=jnp.float32)]
    all_to_all x1 -> x0, starting transfers between devices: 8.09 us -> none  [shards(): lax.all_to_all(residual_in, 'req', split_axis=0, concat_axis=1, tiled=True)]
    dot_general x1 -> x0, local copies, waits for them, and re-layouts: 6.45 us -> none  [shards(): jnp.dot(normed_input, query_weight, preferred_element_type=jnp.float32)]
  transfers between devices with their start and end apart: 4 -> 0, of which waited for: 3 -> 0; matrix products, arithmetic and copies ran while one was open for 3% -> 0% of each run, Pallas kernels for 0% -> 0%
where the time goes in v1:
time: 88.6 us; the launch traced here: 87.2 us
  Pallas kernels  84.4 us (95%)
  other arithmetic  1.5 us (2%)
  local copies, waits for them, and re-layouts  1.38 us (2%)
    pallas_call x1, Pallas kernels, shards(): pl.pallas_call(kernel, out_shape=jax.ShapeDtypeStruct((64, COLS), BF), in...  84.4 us

profile of v1, /device:TPU:0, one launch (start us, length us, event | category | flops | bytes accessed | tf_op | source)
XLA Modules:
  0.0 87.2 jit_solution(12519847397451404880)
XLA Ops:
  0.0 0.7 convert_element_type.3
  0.7 0.1 fusion
  0.8 0.7 pad_maximum_fusion
  1.5 84.4 %shard_map.136 = bf16[64,256]{1,0:T(8,128)(2,1)} custom-call(s32[32]{0:T(128)} %lens.1, bf16[512,256]{1,0:T(8,128)(2,1)} %resid.1, f32[1,4096]{1,0:T(1,128)} %bitcast.6, bf16[4096,512]{1,0:T(8,128)(2,1)} %wq.1, bf16[4096,128]{1,0:T(8,128)(2,1)} %wk.1, bf16[4096,128]{1,0:T(8,128)(2,1)} %wv.1, bf16[32,640,128]{2,1,0:T(8,128)(2,1)} %bitcast.4, ...), custom_call_target="tpu_custom_call" | custom-call | tf_op jit(solution)/shard_map/pallas_call | solution.py:455
  85.9 1.4 %copy.16 = bf16[64,256]{1,0:T(8,128)(2,1)} copy(bf16[64,256]{1,0:T(8,128)(2,1)} %shard_map.136) | data formatting | bytes 65536
  (1 shorter events, 0.0 us)

commit v2 on v0

v2 whole, which is shorter than its diff:
```python
import functools
import math

import jax
import jax.numpy as jnp
from jax import lax
from jax.experimental import pallas as pl
from jax.experimental.pallas import tpu as pltpu
from jax.sharding import PartitionSpec as P

MODEL_WIDTH = 4096
WINDOW = 512
SINKS = 4
EPS = 1e-05
THETA = 10000.0

NR = 16
NK = 8
ROWS = 32
COLS = 256
FFK = 1792
HEADS = 4
HD = 128
SLOTS = 640
CHUNK = 896

BF = jnp.bfloat16
F32 = jnp.float32
MESH = pl.DeviceIdType.MESH
NT = (((1,), (1,)), ((), ()))
TN = (((0,), (0,)), ((), ()))


def dot(a, b):
    return jnp.dot(a, b, preferred_element_type=F32)


def piece_offset(l):
    return 448 * l + 64 * (l % 2)


def kernel(
    lens, pos, resid, gain1, wq, wk, wv, kc, vc, wo, gain2, gw, uw, dw,
    out,
    tok, nrm, wq_v, wk_v, wv_v, k_v, v_v, q3, k3, v3, o3, s3, w3, att, attb, wo_v, res_v,
    gp, up, pk, wp, dwp, gl, al, mid, pb, rf, acc, hb, yb, yr, yown, fs, fb, ownf, sqs, sqm,
    ld, tokS, tokR, wS, wR, dS, dR, gS, gR, attS, attR, b2, yS, yR, lS, alR, sqS, sqR,
    rfS, rfR, hS, hR, oS, oR, fS, fR,
):
    r = lax.axis_index("req")
    k = lax.axis_index("kv")
    x, z = r // 4, r % 4
    y, c = k // 2, k % 2
    l = (1 - c) * x + c * z
    m = (1 - c) * z + c * x

    def dev(li, mi):
        return ((1 - c) * (4 * li + mi) + c * (4 * mi + li), k)

    def rc(src, dst, ss, rs, to):
        return pltpu.make_async_remote_copy(
            src_ref=src, dst_ref=dst, send_sem=ss, recv_sem=rs, device_id=to, device_id_type=MESH
        )

    def arrived(ref, sem):
        pltpu.make_async_copy(ref, ref, sem).wait()

    def rows_of(i, n):
        return pl.ds(pl.multiple_of(n * i, n), n)

    barrier = pltpu.get_barrier_semaphore()
    for d in range(1, NR):
        pl.semaphore_signal(barrier, inc=1, device_id=((r + d) % NR, k), device_id_type=MESH)
    for d in range(1, NK):
        pl.semaphore_signal(barrier, inc=1, device_id=(r, (k + d) % NK), device_id_type=MESH)

    loads = {}

    def load(name, src, dst):
        loads[name] = pltpu.make_async_copy(src, dst, ld.at[len(loads)])
        loads[name].start()

    pltpu.make_async_copy(resid.at[rows_of(r, ROWS), :], tok.at[:, rows_of(r, COLS)], tokR).start()
    load("g3", gw.at[:, pl.ds(384, 128)], gp.at[0])
    load("g10", gw.at[:, pl.ds(1280, 128)], gp.at[1])
    load("u3", uw.at[:, pl.ds(384, 128)], up.at[0])
    load("u10", uw.at[:, pl.ds(1280, 128)], up.at[1])
    load("wq", wq, wq_v)
    load("wk", wk, wk_v)
    load("wv", wv, wv_v)
    load("kc", kc, k_v)
    load("vc", vc, v_v)
    load("wo", wo, wo_v)
    load("res", resid.at[rows_of(k, 64), :], res_v)

    pl.semaphore_wait(barrier, NR - 1 + NK - 1)

    for d in range(1, NR):
        to = (r + d) % NR
        rc(resid.at[rows_of(to, ROWS), :], tok.at[:, rows_of(r, COLS)], tokS, tokR, (to, k)).start()
    for d in range(1, NK):
        pl.semaphore_signal(b2, inc=1, device_id=(r, (k + d) % NK), device_id_type=MESH)

    def w_copies(d):
        to = (l + d) % 4
        off = pl.multiple_of(piece_offset(to), 128)
        here = rows_of(l, COLS)
        pieces = (
            (gw.at[:, pl.ds(off, 384)], wp.at[here, pl.ds(0, 384)]),
            (uw.at[:, pl.ds(off, 384)], wp.at[here, pl.ds(384, 384)]),
            (pk.at[to], wp.at[here, pl.ds(768, 128)]),
        )
        if d == 0:
            return [pltpu.make_async_copy(s, t, wR) for s, t in pieces]
        return [rc(s, t, wS, wR, dev(to, m)) for s, t in pieces]

    def d_copies(d):
        to = (l + d) % 4
        off = pl.multiple_of(piece_offset(to), 64)
        off2 = pl.multiple_of(384 + 896 * (to // 2) + 64 * (to % 2), 64)
        here = rows_of(l, COLS)
        pieces = (
            (dw.at[pl.ds(off, 384), :], dwp.at[pl.ds(0, 384), here]),
            (dw.at[pl.ds(off2, 64), :], dwp.at[pl.ds(384, 64), here]),
        )
        if d == 0:
            return [pltpu.make_async_copy(s, t, dR) for s, t in pieces]
        return [rc(s, t, dS, dR, dev(to, m)) for s, t in pieces]

    w_sends = {d: w_copies(d) for d in range(4)}
    for d in (1, 3, 2, 0):
        w_sends[d][0].start()
        w_sends[d][1].start()
    for name in ("g3", "g10", "u3", "u10"):
        loads[name].wait()
    low = lax.broadcasted_iota(jnp.int32, (COLS, 128), 1) < 64
    for t in range(2):
        g = gp[t].astype(F32)
        u = up[t].astype(F32)
        pk[2 * t] = jnp.where(low, g, pltpu.roll(u, 64, 1)).astype(BF)
        pk[2 * t + 1] = jnp.where(low, pltpu.roll(g, 64, 1), u).astype(BF)
    for d in (1, 3, 2, 0):
        w_sends[d][2].start()
    gl[l] = gain2[...]
    for d in range(1, 4):
        rc(gain2, gl.at[l], gS.at[d - 1], gR.at[l], dev((l + d) % 4, m)).start()
    for d in (1, 3, 2, 0):
        for copy in d_copies(d):
            copy.start()

    q3[...] = jnp.zeros_like(q3)
    k3[...] = jnp.zeros_like(k3)
    v3[...] = jnp.zeros_like(v3)
    dwp[448:512, :] = jnp.zeros((64, 1024), BF)

    sub = lax.broadcasted_iota(jnp.int32, (8, 128), 0)
    lane = lax.broadcasted_iota(jnp.int32, (ROWS, HD), 1)
    p8 = jnp.broadcast_to(pos[...].astype(F32), (8, ROWS))
    place = lax.dot_general(
        p8, (sub == 0).astype(F32), TN, preferred_element_type=F32, precision=lax.Precision.HIGHEST
    )
    freq = jnp.exp((lane % 64).astype(F32) * (-2.0 * math.log(THETA) / HD))
    angle = place * freq
    cs = jnp.cos(angle)
    sn = jnp.where(lane < 64, -1.0, 1.0) * jnp.sin(angle)

    arrived(tok, tokR)
    t = tok[...].astype(F32)
    scale = 1.0 / jnp.sqrt(jnp.sum(t * t, axis=-1, keepdims=True) / MODEL_WIDTH + EPS)
    nrm[...] = (t * scale * gain1[...]).astype(BF)
    loads["wq"].wait()
    loads["wk"].wait()
    loads["wv"].wait()
    q = dot(nrm[...], wq_v[...])
    kn = dot(nrm[...], wk_v[...])
    vn = dot(nrm[...], wv_v[...])

    def rotate(v):
        return (v * cs + pltpu.roll(v, 64, 1) * sn).astype(BF).astype(F32)

    kn = rotate(kn)
    vn = vn.astype(BF).astype(F32)
    for h in range(HEADS):
        q3[pl.ds(h, ROWS, stride=8), :] = rotate(q[:, HD * h : HD * (h + 1)])
        k3[pl.ds(h, ROWS, stride=8), :] = kn
        v3[pl.ds(h, ROWS, stride=8), :] = vn

    factor = 1.0 / math.sqrt(HD)
    slot = lax.broadcasted_iota(jnp.int32, (8, SLOTS), 1)
    loads["kc"].wait()
    for half in range(2):
        for b in range(16 * half, 16 * half + 16):
            rows = slice(8 * b, 8 * b + 8)
            s = lax.dot_general(q3[rows, :].astype(BF), k_v[b], NT, preferred_element_type=F32)
            n = lens[b]
            ok = (slot < n) & ((slot < SINKS) | (slot > n - WINDOW))
            s3[rows, :] = jnp.where(ok, s * factor, -1e30)
        rows = slice(128 * half, 128 * half + 128)
        s = s3[rows, :]
        own = jnp.sum(q3[rows, :] * k3[rows, :], axis=-1, keepdims=True) * factor
        peak = jnp.maximum(jnp.max(s, axis=-1, keepdims=True), own)
        e = jnp.where(s > -1e29, jnp.exp(s - peak), 0.0)
        eo = jnp.exp(own - peak)
        inv = 1.0 / (jnp.sum(e, axis=-1, keepdims=True) + eo)
        w3[rows, :] = e * inv
        o3[rows, :] = (eo * inv).astype(BF).astype(F32) * v3[rows, :]
        if half == 0:
            loads["vc"].wait()
        for b in range(16 * half, 16 * half + 16):
            rows = slice(8 * b, 8 * b + 8)
            o3[rows, :] += dot(w3[rows, :].astype(BF), v_v[b])
    for h in range(HEADS):
        att[:, HD * h : HD * (h + 1)] = o3[pl.ds(h, ROWS, stride=8), :].astype(BF)

    kd = r // 2
    there = attb.at[rows_of(r % 2, ROWS), rows_of(k, 512)]
    pl.semaphore_wait(b2, NK - 1)

    @pl.when(k == kd)
    def _():
        pltpu.make_async_copy(att, there, attR).start()

    @pl.when(k != kd)
    def _():
        rc(att, there, attS, attR, (r, kd)).start()

    for d in range(1, NR):
        rc(att, there, attS, attR, ((r + d) % NR, kd)).start()

    arrived(tok.at[:, pl.ds(0, COLS * 15)], tokS)
    arrived(wp.at[pl.ds(0, 768), :], wS)
    for d in range(1, 4):
        rc(gain2, gl.at[l], gS.at[d - 1], gR.at[l], dev((l + d) % 4, m)).wait_send()
    arrived(dwp.at[pl.ds(0, 448), pl.ds(0, 768)], dS)

    loads["wo"].wait()
    loads["res"].wait()
    arrived(attb, attR)
    o = res_v[...].astype(F32) + dot(attb[...], wo_v[...])
    mid[...] = o
    blk = rows_of(k, 64)
    al[blk, rows_of(l, COLS)] = (o * gain2[...]).astype(BF)

    def peer(d):
        return 2 * ((y + d // 2) % 4) + (c + d % 2) % 2

    for i, d in enumerate((1, 2, 3, 6, 7, 4, 5)):
        kp = peer(d)
        cp = kp % 2
        lp = (1 - cp) * x + cp * z
        rc(al.at[blk, rows_of(l, COLS)], al.at[blk, rows_of(lp, COLS)], yS, yR.at[k], (r, kp)).start()
    mycols = rows_of(l, COLS)

    @pl.when(k == kd)
    def _():
        arrived(attb.at[pl.ds(0, 32), pl.ds(0, 3584)], attS)
        arrived(attb.at[pl.ds(32, 32), pl.ds(0, 4096)], attS)

    @pl.when(k != kd)
    def _():
        arrived(attb, attS)

    for i, d in enumerate((0, 1, 3, 2)):
        yp = (y + d) % 4
        for h in range(2):
            kp = 2 * yp + (c + h) % 2
            if d or h:
                arrived(al.at[rows_of(kp, 64), mycols], yR.at[kp])
        at = rows_of(yp, 128)
        for e in (1, 3, 2):
            rc(al.at[at, mycols], al.at[at, mycols], lS, alR.at[l, yp], dev((l + e) % 4, m)).start()

    arrived(wp, wR)
    for d in range(1, 4):
        at = (l + d) % 4
        arrived(gl.at[at], gR.at[at])
    ginv = [1.0 / gl[i] for i in range(4)]
    for i, d in enumerate((0, 1, 3, 2)):
        mi = (y + d) % 4
        at = rows_of(mi, 128)
        for e in (1, 3, 2):
            lp = (l + e) % 4
            arrived(al.at[at, rows_of(lp, COLS)], alR.at[lp, mi])
        p = dot(al[at, :], wp[...])
        part = jnp.zeros((128, 128), F32)
        for j in range(8):
            g = ginv[j // 2][:, 128 * (j % 2) : 128 * (j % 2) + 128]
            v = al[at, 128 * j : 128 * (j + 1)].astype(F32) * g
            part = part + v * v
        sqs[i] = lax.dot_general(
            jnp.ones((8, 128), F32), part, NT, preferred_element_type=F32, precision=lax.Precision.HIGHEST
        )

        @pl.when(mi == m)
        def _():
            acc[...] = p
            sqm[m] = sqs[i]

        @pl.when(mi != m)
        def _():
            pb[i] = p.astype(BF)
            rc(pb.at[i], rf.at[m], rfS.at[i], rfR.at[m], dev(l, mi)).start()
            rc(sqs.at[i], sqm.at[m], sqS.at[i], sqR.at[m], dev(l, mi)).start()

    arrived(al.at[pl.ds(0, 448), pl.ds(0, COLS)], yS)
    arrived(al.at[:, pl.ds(0, 768)], lS)

    for d in (1, 3, 2):
        at = (m + d) % 4
        arrived(sqm.at[at], sqR.at[at])
    sq = sqm[0] + sqm[1] + sqm[2] + sqm[3]
    total = lax.dot_general(
        sq, (sub == 0).astype(F32), TN, preferred_element_type=F32, precision=lax.Precision.HIGHEST
    )
    inv = 1.0 / jnp.sqrt(total / MODEL_WIDTH + EPS)
    for d in (1, 3, 2):
        at = (m + d) % 4
        arrived(rf.at[at], rfR.at[at])
        acc[...] += rf[at].astype(F32)
    mine = rows_of(m, 128)

    def tile(i):
        return acc[:, 128 * i : 128 * (i + 1)] * inv

    def silu(v):
        return v / (1.0 + jnp.exp(-v))

    for i in range(3):
        hb[mine, 128 * i : 128 * (i + 1)] = (silu(tile(i)) * tile(3 + i)).astype(BF)
    t = tile(6)
    low = lax.broadcasted_iota(jnp.int32, (128, 128), 1) < 64
    hb[mine, 384:512] = jnp.where(low, silu(t) * pltpu.roll(t, 64, 1), 0.0).astype(BF)

    for e in (1, 3, 2):
        rc(hb.at[mine, :], hb.at[mine, :], hS, hR.at[m], dev(l, (m + e) % 4)).start()
    for i, d in enumerate((0, 1, 3, 2)):
        mi = (y + d) % 4

        @pl.when(mi != m)
        def _():
            rc(pb.at[i], rf.at[m], rfS.at[i], rfR.at[m], dev(l, mi)).wait_send()
            rc(sqs.at[i], sqm.at[m], sqS.at[i], sqR.at[m], dev(l, mi)).wait_send()

    arrived(dwp.at[pl.ds(0, 448), :], dR)

    def y_copy(e, mi):
        to = (l + e) % 4
        at = rows_of(mi, 128)
        return rc(yb.at[at, rows_of(to, COLS)], yr.at[l, at, :], oS, oR.at[l, mi], dev(to, m))

    def last_copy(kp):
        return rc(fs.at[kp], fb.at[k], fS, fR.at[k], (r, kp))

    def finish(mi):
        at = rows_of(mi, 128)
        v = yown[at, :]
        for e in (1, 3, 2):
            lp = (l + e) % 4
            arrived(yr.at[lp, at, :], oR.at[lp, mi])
            v = v + yr[lp, at, :].astype(F32)
        for i in range(2):
            kp = 2 * mi + i
            fs[kp] = v[64 * i : 64 * (i + 1), :].astype(BF)

            @pl.when(kp == k)
            def _():
                ownf[...] = v[64 * i : 64 * (i + 1), :]

            @pl.when(kp != k)
            def _():
                last_copy(kp).start()

    turns = [(m + d) % 4 for d in (0, 1, 3, 2)]
    for i, mi in enumerate(turns):
        at = rows_of(mi, 128)
        if i:
            arrived(hb.at[at, :], hR.at[mi])
        v = dot(hb[at, :], dwp[...])
        yb[at, :] = v.astype(BF)
        for e in (1, 3, 2):
            y_copy(e, mi).start()
        yown[at, :] = dot(hb[at, :], dwp[:, rows_of(l, COLS)])
    for mi in turns:
        finish(mi)

    arrived(hb.at[pl.ds(0, 384), :], hS)
    arrived(yb.at[:, pl.ds(0, 768)], oS)
    res = mid[...] + ownf[...]
    for d in (1, 2, 3, 6, 7, 4, 5):
        kp = peer(d)
        arrived(fb.at[kp], fR.at[kp])
        res = res + fb[kp].astype(F32)
    out[...] = res.astype(BF)
    arrived(fs.at[pl.ds(0, 7)], fS)


def shards(
    residual_in,
    attn_gain,
    query_weight,
    key_matrix,
    value_matrix,
    key_cache,
    cached_values,
    cache_lengths,
    positions,
    output_weight,
    mlp_gain,
    gate_weight,
    up_weight,
    down_weight,
):
    hbm = pl.BlockSpec(memory_space=pltpu.MemorySpace.HBM)
    vmem = pl.BlockSpec(memory_space=pltpu.MemorySpace.VMEM)
    smem = pl.BlockSpec(memory_space=pltpu.MemorySpace.SMEM)
    V = pltpu.VMEM
    dma = lambda *shape: pltpu.SemaphoreType.DMA(shape) if shape else pltpu.SemaphoreType.DMA
    return pl.pallas_call(
        kernel,
        out_shape=jax.ShapeDtypeStruct((64, COLS), BF),
        in_specs=[smem, vmem, hbm, vmem, hbm, hbm, hbm, hbm, hbm, hbm, vmem, hbm, hbm, hbm],
        out_specs=vmem,
        scratch_shapes=[
            V((ROWS, MODEL_WIDTH), BF),
            V((ROWS, MODEL_WIDTH), BF),
            V((MODEL_WIDTH, HEADS * HD), BF),
            V((MODEL_WIDTH, HD), BF),
            V((MODEL_WIDTH, HD), BF),
            V((ROWS, SLOTS, HD), BF),
            V((ROWS, SLOTS, HD), BF),
            V((8 * ROWS, HD), F32),
            V((8 * ROWS, HD), F32),
            V((8 * ROWS, HD), F32),
            V((8 * ROWS, HD), F32),
            V((8 * ROWS, SLOTS), F32),
            V((8 * ROWS, SLOTS), F32),
            V((ROWS, HEADS * HD), BF),
            V((64, MODEL_WIDTH), BF),
            V((MODEL_WIDTH, COLS), BF),
            V((64, COLS), BF),
            V((2, COLS, 128), BF),
            V((2, COLS, 128), BF),
            V((4, COLS, 128), BF),
            V((1024, CHUNK), BF),
            V((512, 1024), BF),
            V((4, 1, COLS), F32),
            V((512, 1024), BF),
            V((64, COLS), F32),
            V((4, 128, CHUNK), BF),
            V((4, 128, CHUNK), BF),
            V((128, CHUNK), F32),
            V((512, 512), BF),
            V((512, 1024), BF),
            V((4, 512, COLS), BF),
            V((512, COLS), F32),
            V((NK, 64, COLS), BF),
            V((NK, 64, COLS), BF),
            V((64, COLS), F32),
            V((4, 8, 128), F32),
            V((4, 8, 128), F32),
            dma(11),
            dma(),
            dma(),
            dma(),
            dma(),
            dma(),
            dma(),
            dma(3),
            dma(4),
            dma(),
            dma(),
            pltpu.SemaphoreType.REGULAR,
            dma(),
            dma(NK),
            dma(),
            dma(4, 4),
            dma(4),
            dma(4),
            dma(4),
            dma(4),
            dma(),
            dma(4),
            dma(),
            dma(4, 4),
            dma(),
            dma(NK),
        ],
        compiler_params=pltpu.CompilerParams(
            collective_id=0, has_side_effects=True, vmem_limit_bytes=56 << 20
        ),
    )(
        cache_lengths,
        positions.reshape(1, ROWS),
        residual_in,
        attn_gain.reshape(1, MODEL_WIDTH),
        query_weight,
        key_matrix,
        value_matrix,
        key_cache.reshape(ROWS, SLOTS, HD),
        cached_values.reshape(ROWS, SLOTS, HD),
        output_weight,
        mlp_gain.reshape(1, COLS),
        gate_weight,
        up_weight,
        down_weight,
    )


def solution(mesh):
    return jax.shard_map(
        shards,
        mesh=mesh,
        in_specs=(
            P(None, "req"),
            P(),
            P(None, "kv"),
            P(None, "kv"),
            P(None, "kv"),
            P("req", "kv", None, None),
            P("req", "kv", None, None),
            P("req"),
            P("req"),
            P(None, "req"),
            P("req"),
            P("req", "kv"),
            P("req", "kv"),
            P("kv", "req"),
        ),
        out_specs=P("kv", "req"),
        check_vma=False,
    )
```

time: 267 us -> 81.6 us (0.31)
  the two profiles are of different devices: /device:TPU:0 before, /device:TPU:21 now
where the time goes in v2:
time: 81.6 us; the launch traced here: 81.4 us
  Pallas kernels  80 us (98%)
  local copies, waits for them, and re-layouts  1.38 us (2%)
    pallas_call x1, Pallas kernels, shards(): pl.pallas_call(kernel, out_shape=jax.ShapeDtypeStruct((64, COLS), BF), in...  80 us

profile of v2, /device:TPU:21, one launch (start us, length us, event | category | flops | bytes accessed | tf_op | source)
XLA Modules:
  0.0 81.4 jit_solution(10976734970486995571)
XLA Ops:
  0.0 80.0 %shard_map.136 = bf16[64,256]{1,0:T(8,128)(2,1)} custom-call(s32[32]{0:T(128)} %lens.1, s32[1,32]{1,0:T(1,128)} %bitcast.9, bf16[512,256]{1,0:T(8,128)(2,1)} %resid.1, f32[1,4096]{1,0:T(1,128)} %bitcast.7, bf16[4096,512]{1,0:T(8,128)(2,1)} %wq.1, bf16[4096,128]{1,0:T(8,128)(2,1)} %wk.1, bf16[4096,128]{1,0:T(8,128)(2,1)} %wv.1, ...), custom_call_target="tpu_custom_call" | custom-call | tf_op jit(solution)/shard_map/pallas_call | solution.py:418
  80.0 1.4 %copy.16 = bf16[64,256]{1,0:T(8,128)(2,1)} copy(bf16[64,256]{1,0:T(8,128)(2,1)} %shard_map.136) | data formatting | bytes 65536

commit v3 on v2

--- a/solution.py
+++ b/solution.py
@@ -18,7 +18,6 @@
 NK = 8
 ROWS = 32
 COLS = 256
-FFK = 1792
 HEADS = 4
 HD = 128
 SLOTS = 640
@@ -43,7 +42,7 @@
     lens, pos, resid, gain1, wq, wk, wv, kc, vc, wo, gain2, gw, uw, dw,
     out,
     tok, nrm, wq_v, wk_v, wv_v, k_v, v_v, q3, k3, v3, o3, s3, w3, att, attb, wo_v, res_v,
-    gp, up, pk, wp, dwp, gl, al, mid, pb, rf, acc, hb, yb, yr, yown, fs, fb, ownf, sqs, sqm,
+    gp, up, pk, wp, dwp, gl, al, mid, pb, rf, hb, yb, yr, fs, fb, invs, sqm,
     ld, tokS, tokR, wS, wR, dS, dR, gS, gR, attS, attR, b2, yS, yR, lS, alR, sqS, sqR,
     rfS, rfR, hS, hR, oS, oR, fS, fR,
 ):
@@ -144,9 +143,6 @@
     gl[l] = gain2[...]
     for d in range(1, 4):
         rc(gain2, gl.at[l], gS.at[d - 1], gR.at[l], dev((l + d) % 4, m)).start()
-    for d in (1, 3, 2, 0):
-        for copy in d_copies(d):
-            copy.start()
 
     q3[...] = jnp.zeros_like(q3)
     k3[...] = jnp.zeros_like(k3)
@@ -231,25 +227,43 @@
     arrived(wp.at[pl.ds(0, 768), :], wS)
     for d in range(1, 4):
         rc(gain2, gl.at[l], gS.at[d - 1], gR.at[l], dev((l + d) % 4, m)).wait_send()
-    arrived(dwp.at[pl.ds(0, 448), pl.ds(0, 768)], dS)
 
     loads["wo"].wait()
     loads["res"].wait()
     arrived(attb, attR)
+    for d in (1, 3, 2, 0):
+        for copy in d_copies(d):
+            copy.start()
     o = res_v[...].astype(F32) + dot(attb[...], wo_v[...])
     mid[...] = o
-    blk = rows_of(k, 64)
-    al[blk, rows_of(l, COLS)] = (o * gain2[...]).astype(BF)
-
-    def peer(d):
-        return 2 * ((y + d // 2) % 4) + (c + d % 2) % 2
-
-    for i, d in enumerate((1, 2, 3, 6, 7, 4, 5)):
-        kp = peer(d)
+    mine = rows_of(y, 64)
+    mycols = rows_of(l, COLS)
+    al[c, mine, mycols] = (o * gain2[...]).astype(BF)
+
+    around = (1, 3, 2)
+
+    def kv_send(kp):
         cp = kp % 2
         lp = (1 - cp) * x + cp * z
-        rc(al.at[blk, rows_of(l, COLS)], al.at[blk, rows_of(lp, COLS)], yS, yR.at[k], (r, kp)).start()
-    mycols = rows_of(l, COLS)
+        rc(al.at[c, mine, mycols], al.at[c, mine, rows_of(lp, COLS)], yS, yR.at[k], (r, kp)).start()
+
+    def line_sends(h, yp):
+        block = al.at[h, rows_of(yp, 64), mycols]
+        for e in around:
+            rc(block, block, lS, alR.at[h, l], dev((l + e) % 4, m)).start()
+
+    halves = (c, 1 - c)
+    for e in around:
+        kv_send(2 * ((y + e) % 4) + c)
+    for e in (0,) + around:
+        kv_send(2 * ((y + e) % 4) + 1 - c)
+    line_sends(c, y)
+    for i, h in enumerate(halves):
+        for e in around if i == 0 else (0,) + around:
+            yp = (y + e) % 4
+            kp = 2 * yp + h
+            arrived(al.at[h, rows_of(yp, 64), mycols], yR.at[kp])
+            line_sends(h, yp)
 
     @pl.when(k == kd)
     def _():
@@ -259,139 +273,115 @@
     @pl.when(k != kd)
     def _():
         arrived(attb, attS)
-
-    for i, d in enumerate((0, 1, 3, 2)):
-        yp = (y + d) % 4
-        for h in range(2):
-            kp = 2 * yp + (c + h) % 2
-            if d or h:
-                arrived(al.at[rows_of(kp, 64), mycols], yR.at[kp])
-        at = rows_of(yp, 128)
-        for e in (1, 3, 2):
-            rc(al.at[at, mycols], al.at[at, mycols], lS, alR.at[l, yp], dev((l + e) % 4, m)).start()
 
     arrived(wp, wR)
     for d in range(1, 4):
         at = (l + d) % 4
         arrived(gl.at[at], gR.at[at])
     ginv = [1.0 / gl[i] for i in range(4)]
-    for i, d in enumerate((0, 1, 3, 2)):
-        mi = (y + d) % 4
-        at = rows_of(mi, 128)
-        for e in (1, 3, 2):
+    my64 = rows_of(m, 64)
+
+    def gate(h):
+        for e in around:
             lp = (l + e) % 4
-            arrived(al.at[at, rows_of(lp, COLS)], alR.at[lp, mi])
-        p = dot(al[at, :], wp[...])
-        part = jnp.zeros((128, 128), F32)
+            arrived(al.at[h, :, rows_of(lp, COLS)], alR.at[h, lp])
+        pb[h] = dot(al[h], wp[...]).astype(BF)
+        for e in around:
+            mi = (m + e) % 4
+            rc(pb.at[h, rows_of(mi, 64), :], rf.at[h, m], rfS, rfR.at[h, m], dev(l, mi)).start()
+        part = jnp.zeros((256, 128), F32)
         for j in range(8):
             g = ginv[j // 2][:, 128 * (j % 2) : 128 * (j % 2) + 128]
-            v = al[at, 128 * j : 128 * (j + 1)].astype(F32) * g
+            v = al[h, :, 128 * j : 128 * (j + 1)].astype(F32) * g
             part = part + v * v
-        sqs[i] = lax.dot_general(
+        sqm[h, m] = lax.dot_general(
             jnp.ones((8, 128), F32), part, NT, preferred_element_type=F32, precision=lax.Precision.HIGHEST
         )
-
-        @pl.when(mi == m)
-        def _():
-            acc[...] = p
-            sqm[m] = sqs[i]
-
-        @pl.when(mi != m)
-        def _():
-            pb[i] = p.astype(BF)
-            rc(pb.at[i], rf.at[m], rfS.at[i], rfR.at[m], dev(l, mi)).start()
-            rc(sqs.at[i], sqm.at[m], sqS.at[i], sqR.at[m], dev(l, mi)).start()
-
-    arrived(al.at[pl.ds(0, 448), pl.ds(0, COLS)], yS)
-    arrived(al.at[:, pl.ds(0, 768)], lS)
-
-    for d in (1, 3, 2):
-        at = (m + d) % 4
-        arrived(sqm.at[at], sqR.at[at])
-    sq = sqm[0] + sqm[1] + sqm[2] + sqm[3]
-    total = lax.dot_general(
-        sq, (sub == 0).astype(F32), TN, preferred_element_type=F32, precision=lax.Precision.HIGHEST
-    )
-    inv = 1.0 / jnp.sqrt(total / MODEL_WIDTH + EPS)
-    for d in (1, 3, 2):
-        at = (m + d) % 4
-        arrived(rf.at[at], rfR.at[at])
-        acc[...] += rf[at].astype(F32)
-    mine = rows_of(m, 128)
-
-    def tile(i):
-        return acc[:, 128 * i : 128 * (i + 1)] * inv
+        for e in around:
+            mi = (m + e) % 4
+            rc(sqm.at[h, m], sqm.at[h, m], sqS, sqR.at[h, m], dev(l, mi)).start()
 
     def silu(v):
         return v / (1.0 + jnp.exp(-v))
 
-    for i in range(3):
-        hb[mine, 128 * i : 128 * (i + 1)] = (silu(tile(i)) * tile(3 + i)).astype(BF)
-    t = tile(6)
-    low = lax.broadcasted_iota(jnp.int32, (128, 128), 1) < 64
-    hb[mine, 384:512] = jnp.where(low, silu(t) * pltpu.roll(t, 64, 1), 0.0).astype(BF)
-
-    for e in (1, 3, 2):
-        rc(hb.at[mine, :], hb.at[mine, :], hS, hR.at[m], dev(l, (m + e) % 4)).start()
-    for i, d in enumerate((0, 1, 3, 2)):
-        mi = (y + d) % 4
-
-        @pl.when(mi != m)
-        def _():
-            rc(pb.at[i], rf.at[m], rfS.at[i], rfR.at[m], dev(l, mi)).wait_send()
-            rc(sqs.at[i], sqm.at[m], sqS.at[i], sqR.at[m], dev(l, mi)).wait_send()
-
+    def hide(h):
+        for e in around:
+            mi = (m + e) % 4
+            arrived(sqm.at[h, mi], sqR.at[h, mi])
+        total = lax.dot_general(
+            sqm[h, 0] + sqm[h, 1] + sqm[h, 2] + sqm[h, 3],
+            (sub == 0).astype(F32),
+            TN,
+            preferred_element_type=F32,
+            precision=lax.Precision.HIGHEST,
+        )
+        invs[...] = 1.0 / jnp.sqrt(total / MODEL_WIDTH + EPS)
+        inv = invs[my64, :]
+        for e in around:
+            mi = (m + e) % 4
+            arrived(rf.at[h, mi], rfR.at[h, mi])
+
+        def tile(i):
+            at = slice(128 * i, 128 * (i + 1))
+            v = pb[h, my64, at].astype(F32)
+            for e in around:
+                v = v + rf[h, (m + e) % 4, :, at].astype(F32)
+            return v * inv
+
+        for i in range(3):
+            hb[h, my64, 128 * i : 128 * (i + 1)] = (silu(tile(i)) * tile(3 + i)).astype(BF)
+        t = tile(6)
+        low = lax.broadcasted_iota(jnp.int32, (64, 128), 1) < 64
+        hb[h, my64, 384:512] = jnp.where(low, silu(t) * pltpu.roll(t, 64, 1), 0.0).astype(BF)
+        for e in around:
+            rc(hb.at[h, my64, :], hb.at[h, my64, :], hS, hR.at[h, m], dev(l, (m + e) % 4)).start()
+
+    for h in halves:
+        gate(h)
+    for h in halves:
+        hide(h)
+
+    arrived(hb.at[0, pl.ds(0, 224), :], yS)
+    arrived(al.at[:, :, pl.ds(0, 768)], lS)
+    arrived(pb.at[:, pl.ds(0, 192), :], rfS)
+    arrived(sqm.at[:, pl.ds(0, 3)], sqS)
+    arrived(dwp.at[pl.ds(0, 448), pl.ds(0, 768)], dS)
     arrived(dwp.at[pl.ds(0, 448), :], dR)
 
-    def y_copy(e, mi):
-        to = (l + e) % 4
-        at = rows_of(mi, 128)
-        return rc(yb.at[at, rows_of(to, COLS)], yr.at[l, at, :], oS, oR.at[l, mi], dev(to, m))
-
-    def last_copy(kp):
-        return rc(fs.at[kp], fb.at[k], fS, fR.at[k], (r, kp))
-
-    def finish(mi):
-        at = rows_of(mi, 128)
-        v = yown[at, :]
-        for e in (1, 3, 2):
+    def down(h):
+        for e in around:
+            mi = (m + e) % 4
+            arrived(hb.at[h, rows_of(mi, 64), :], hR.at[h, mi])
+        yb[h] = dot(hb[h], dwp[...]).astype(BF)
+        for e in around:
+            to = (l + e) % 4
+            rc(yb.at[h, :, rows_of(to, COLS)], yr.at[h, l], oS, oR.at[h, l], dev(to, m)).start()
+
+    def finish(i, h):
+        v = yb[h, :, mycols].astype(F32)
+        for e in around:
             lp = (l + e) % 4
-            arrived(yr.at[lp, at, :], oR.at[lp, mi])
-            v = v + yr[lp, at, :].astype(F32)
-        for i in range(2):
-            kp = 2 * mi + i
-            fs[kp] = v[64 * i : 64 * (i + 1), :].astype(BF)
-
-            @pl.when(kp == k)
-            def _():
-                ownf[...] = v[64 * i : 64 * (i + 1), :]
-
-            @pl.when(kp != k)
-            def _():
-                last_copy(kp).start()
-
-    turns = [(m + d) % 4 for d in (0, 1, 3, 2)]
-    for i, mi in enumerate(turns):
-        at = rows_of(mi, 128)
-        if i:
-            arrived(hb.at[at, :], hR.at[mi])
-        v = dot(hb[at, :], dwp[...])
-        yb[at, :] = v.astype(BF)
-        for e in (1, 3, 2):
-            y_copy(e, mi).start()
-        yown[at, :] = dot(hb[at, :], dwp[:, rows_of(l, COLS)])
-    for mi in turns:
-        finish(mi)
-
-    arrived(hb.at[pl.ds(0, 384), :], hS)
-    arrived(yb.at[:, pl.ds(0, 768)], oS)
-    res = mid[...] + ownf[...]
-    for d in (1, 2, 3, 6, 7, 4, 5):
-        kp = peer(d)
-        arrived(fb.at[kp], fR.at[kp])
-        res = res + fb[kp].astype(F32)
+            arrived(yr.at[h, lp], oR.at[h, lp])
+            v = v + yr[h, lp].astype(F32)
+        fs[h] = v.astype(BF)
+        for e in around if i == 0 else (0,) + around:
+            yp = (y + e) % 4
+            rc(fs.at[h, rows_of(yp, 64), :], fb.at[k], fS, fR.at[k], (r, 2 * yp + h)).start()
+
+    for h in halves:
+        down(h)
+    for i, h in enumerate(halves):
+        finish(i, h)
+    arrived(hb.at[:, pl.ds(0, 192), :], hS)
+    arrived(yb.at[:, :, pl.ds(0, 768)], oS)
+    res = mid[...] + fs[c, mine, :].astype(F32)
+    for i, h in enumerate(halves):
+        for e in around if i == 0 else (0,) + around:
+            kp = 2 * ((y + e) % 4) + h
+            arrived(fb.at[kp], fR.at[kp])
+            res = res + fb[kp].astype(F32)
     out[...] = res.astype(BF)
-    arrived(fs.at[pl.ds(0, 7)], fS)
+    arrived(yb.at[0, pl.ds(0, 112), :], fS)
 
 
 def shards(
@@ -444,20 +434,17 @@
             V((1024, CHUNK), BF),
             V((512, 1024), BF),
             V((4, 1, COLS), F32),
-            V((512, 1024), BF),
+            V((2, 256, 1024), BF),
             V((64, COLS), F32),
-            V((4, 128, CHUNK), BF),
-            V((4, 128, CHUNK), BF),
-            V((128, CHUNK), F32),
-            V((512, 512), BF),
-            V((512, 1024), BF),
-            V((4, 512, COLS), BF),
-            V((512, COLS), F32),
+            V((2, 256, CHUNK), BF),
+            V((2, 4, 64, CHUNK), BF),
+            V((2, 256, 512), BF),
+            V((2, 256, 1024), BF),
+            V((2, 4, 256, COLS), BF),
+            V((2, 256, COLS), BF),
             V((NK, 64, COLS), BF),
-            V((NK, 64, COLS), BF),
-            V((64, COLS), F32),
-            V((4, 8, 128), F32),
-            V((4, 8, 128), F32),
+            V((256, 128), F32),
+            V((2, 4, 8, 256), F32),
             dma(11),
             dma(),
             dma(),
@@ -473,15 +460,15 @@
             dma(),
             dma(NK),
             dma(),
-            dma(4, 4),
-            dma(4),
-            dma(4),
-            dma(4),
-            dma(4),
-            dma(),
-            dma(4),
-            dma(),
-            dma(4, 4),
+            dma(2, 4),
+            dma(),
+            dma(2, 4),
+            dma(),
+            dma(2, 4),
+            dma(),
+            dma(2, 4),
+            dma(),
+            dma(2, 4),
             dma(),
             dma(NK),
         ],

time: 81.6 us -> 77.5 us (0.950)
  the two profiles are of different devices: /device:TPU:21 before, /device:TPU:1 now
where the time goes in v3:
time: 77.5 us; the launch traced here: 77.3 us
  Pallas kernels  75.9 us (98%)
  local copies, waits for them, and re-layouts  1.38 us (2%)
    pallas_call x1, Pallas kernels, shards(): pl.pallas_call(kernel, out_shape=jax.ShapeDtypeStruct((64, COLS), BF), in...  75.9 us

profile of v3, /device:TPU:1, one launch (start us, length us, event | category | flops | bytes accessed | tf_op | source)
XLA Modules:
  0.0 77.3 jit_solution(9161982106232917035)
XLA Ops:
  0.0 75.9 %shard_map.136 = bf16[64,256]{1,0:T(8,128)(2,1)} custom-call(s32[32]{0:T(128)} %lens.1, s32[1,32]{1,0:T(1,128)} %bitcast.9, bf16[512,256]{1,0:T(8,128)(2,1)} %resid.1, f32[1,4096]{1,0:T(1,128)} %bitcast.7, bf16[4096,512]{1,0:T(8,128)(2,1)} %wq.1, bf16[4096,128]{1,0:T(8,128)(2,1)} %wk.1, bf16[4096,128]{1,0:T(8,128)(2,1)} %wv.1, ...), custom_call_target="tpu_custom_call" | custom-call | tf_op jit(solution)/shard_map/pallas_call | solution.py:408
  75.9 1.4 %copy.16 = bf16[64,256]{1,0:T(8,128)(2,1)} copy(bf16[64,256]{1,0:T(8,128)(2,1)} %shard_map.136) | data formatting | bytes 65536

commit v4 on v3

--- a/solution.py
+++ b/solution.py
@@ -42,9 +42,9 @@
     lens, pos, resid, gain1, wq, wk, wv, kc, vc, wo, gain2, gw, uw, dw,
     out,
     tok, nrm, wq_v, wk_v, wv_v, k_v, v_v, q3, k3, v3, o3, s3, w3, att, attb, wo_v, res_v,
-    gp, up, pk, wp, dwp, gl, al, mid, pb, rf, hb, yb, yr, fs, fb, invs, sqm,
+    gp, up, pk, wp, dwp, gl, al, mid, pb, rf, hb, yb, yr, vf, fs, fb, invs, sqm, mb,
     ld, tokS, tokR, wS, wR, dS, dR, gS, gR, attS, attR, b2, yS, yR, lS, alR, sqS, sqR,
-    rfS, rfR, hS, hR, oS, oR, fS, fR,
+    rfS, rfR, hS, hR, oS, oR, fS, fR, swS, swR, sdS, sdR,
 ):
     r = lax.axis_index("req")
     k = lax.axis_index("kv")
@@ -55,6 +55,14 @@
 
     def dev(li, mi):
         return ((1 - c) * (4 * li + mi) + c * (4 * mi + li), k)
+
+    def places(j):
+        return (1 - j) * x + j * z, (1 - j) * z + j * x
+
+    def devj(j, li, mi):
+        return ((1 - j) * (4 * li + mi) + j * (4 * mi + li), k)
+
+    sibling = (r, 2 * y + 1 - c)
 
     def rc(src, dst, ss, rs, to):
         return pltpu.make_async_remote_copy(
@@ -105,9 +113,9 @@
         off = pl.multiple_of(piece_offset(to), 128)
         here = rows_of(l, COLS)
         pieces = (
-            (gw.at[:, pl.ds(off, 384)], wp.at[here, pl.ds(0, 384)]),
-            (uw.at[:, pl.ds(off, 384)], wp.at[here, pl.ds(384, 384)]),
-            (pk.at[to], wp.at[here, pl.ds(768, 128)]),
+            (gw.at[:, pl.ds(off, 384)], wp.at[c, here, pl.ds(0, 384)]),
+            (uw.at[:, pl.ds(off, 384)], wp.at[c, here, pl.ds(384, 384)]),
+            (pk.at[to], wp.at[c, here, pl.ds(768, 128)]),
         )
         if d == 0:
             return [pltpu.make_async_copy(s, t, wR) for s, t in pieces]
@@ -119,8 +127,8 @@
         off2 = pl.multiple_of(384 + 896 * (to // 2) + 64 * (to % 2), 64)
         here = rows_of(l, COLS)
         pieces = (
-            (dw.at[pl.ds(off, 384), :], dwp.at[pl.ds(0, 384), here]),
-            (dw.at[pl.ds(off2, 64), :], dwp.at[pl.ds(384, 64), here]),
+            (dw.at[pl.ds(off, 384), :], dwp.at[c, pl.ds(0, 384), here]),
+            (dw.at[pl.ds(off2, 64), :], dwp.at[c, pl.ds(384, 64), here]),
         )
         if d == 0:
             return [pltpu.make_async_copy(s, t, dR) for s, t in pieces]
@@ -140,14 +148,25 @@
         pk[2 * t + 1] = jnp.where(low, pltpu.roll(g, 64, 1), u).astype(BF)
     for d in (1, 3, 2, 0):
         w_sends[d][2].start()
-    gl[l] = gain2[...]
-    for d in range(1, 4):
-        rc(gain2, gl.at[l], gS.at[d - 1], gR.at[l], dev((l + d) % 4, m)).start()
+    def gain_copies():
+        out = []
+        for j in range(2):
+            lj, mj = places(j)
+            for d in range(1, 4):
+                to = devj(j, (lj + d) % 4, mj)
+                out.append(rc(gain2, gl.at[j, lj], gS.at[j, d - 1], gR.at[j, lj], to))
+        return out
+
+    for j in range(2):
+        gl[j, places(j)[0]] = gain2[...]
+    for copy in gain_copies():
+        copy.start()
 
     q3[...] = jnp.zeros_like(q3)
     k3[...] = jnp.zeros_like(k3)
     v3[...] = jnp.zeros_like(v3)
-    dwp[448:512, :] = jnp.zeros((64, 1024), BF)
+    for j in range(2):
+        dwp[j, 448:512, :] = jnp.zeros((64, 1024), BF)
 
     sub = lax.broadcasted_iota(jnp.int32, (8, 128), 0)
     lane = lax.broadcasted_iota(jnp.int32, (ROWS, HD), 1)
@@ -224,9 +243,9 @@
         rc(att, there, attS, attR, ((r + d) % NR, kd)).start()
 
     arrived(tok.at[:, pl.ds(0, COLS * 15)], tokS)
-    arrived(wp.at[pl.ds(0, 768), :], wS)
-    for d in range(1, 4):
-        rc(gain2, gl.at[l], gS.at[d - 1], gR.at[l], dev((l + d) % 4, m)).wait_send()
+    arrived(wp.at[c, pl.ds(0, 768), :], wS)
+    for copy in gain_copies():
+        copy.wait_send()
 
     loads["wo"].wait()
     loads["res"].wait()
@@ -234,36 +253,34 @@
     for d in (1, 3, 2, 0):
         for copy in d_copies(d):
             copy.start()
+    arrived(wp.at[c], wR)
+    rc(wp.at[c], wp.at[c], swS, swR, sibling).start()
     o = res_v[...].astype(F32) + dot(attb[...], wo_v[...])
     mid[...] = o
     mine = rows_of(y, 64)
-    mycols = rows_of(l, COLS)
-    al[c, mine, mycols] = (o * gain2[...]).astype(BF)
+    mb[mine, :] = (o * gain2[...]).astype(BF)
 
     around = (1, 3, 2)
-
-    def kv_send(kp):
-        cp = kp % 2
-        lp = (1 - cp) * x + cp * z
-        rc(al.at[c, mine, mycols], al.at[c, mine, rows_of(lp, COLS)], yS, yR.at[k], (r, kp)).start()
-
-    def line_sends(h, yp):
-        block = al.at[h, rows_of(yp, 64), mycols]
-        for e in around:
-            rc(block, block, lS, alR.at[h, l], dev((l + e) % 4, m)).start()
-
-    halves = (c, 1 - c)
+    sets = (c, 1 - c)
+
+    def line_sends(j, yp):
+        lj, mj = places(j)
+        at = rows_of(yp, 64)
+        for e in around:
+            rc(mb.at[at, :], al.at[j, at, rows_of(lj, COLS)], lS, alR.at[j, lj], devj(j, (lj + e) % 4, mj)).start()
+
     for e in around:
-        kv_send(2 * ((y + e) % 4) + c)
-    for e in (0,) + around:
-        kv_send(2 * ((y + e) % 4) + 1 - c)
-    line_sends(c, y)
-    for i, h in enumerate(halves):
-        for e in around if i == 0 else (0,) + around:
+        rc(mb.at[mine, :], mb.at[mine, :], yS, yR.at[y], (r, 2 * ((y + e) % 4) + c)).start()
+    for j in sets:
+        line_sends(j, y)
+    for i, j in enumerate(sets):
+        for e in around:
             yp = (y + e) % 4
-            kp = 2 * yp + h
-            arrived(al.at[h, rows_of(yp, 64), mycols], yR.at[kp])
-            line_sends(h, yp)
+            if i == 0:
+                arrived(mb.at[rows_of(yp, 64), :], yR.at[yp])
+            line_sends(j, yp)
+    for j in range(2):
+        al[j, :, rows_of(places(j)[0], COLS)] = mb[...]
 
     @pl.when(k == kd)
     def _():
@@ -274,114 +291,118 @@
     def _():
         arrived(attb, attS)
 
-    arrived(wp, wR)
-    for d in range(1, 4):
-        at = (l + d) % 4
-        arrived(gl.at[at], gR.at[at])
-    ginv = [1.0 / gl[i] for i in range(4)]
-    my64 = rows_of(m, 64)
-
-    def gate(h):
-        for e in around:
-            lp = (l + e) % 4
-            arrived(al.at[h, :, rows_of(lp, COLS)], alR.at[h, lp])
-        pb[h] = dot(al[h], wp[...]).astype(BF)
-        for e in around:
-            mi = (m + e) % 4
-            rc(pb.at[h, rows_of(mi, 64), :], rf.at[h, m], rfS, rfR.at[h, m], dev(l, mi)).start()
+    def silu(v):
+        return v / (1.0 + jnp.exp(-v))
+
+    def gate(j):
+        lj, mj = places(j)
+        for e in around:
+            lp = (lj + e) % 4
+            arrived(al.at[j, :, rows_of(lp, COLS)], alR.at[j, lp])
+        pb[j] = dot(al[j], wp[j]).astype(BF)
+        for e in around:
+            mi = (mj + e) % 4
+            rc(pb.at[j, rows_of(mi, 64), :], rf.at[j, mj], rfS, rfR.at[j, mj], devj(j, lj, mi)).start()
+        for e in around:
+            at = (lj + e) % 4
+            arrived(gl.at[j, at], gR.at[j, at])
         part = jnp.zeros((256, 128), F32)
-        for j in range(8):
-            g = ginv[j // 2][:, 128 * (j % 2) : 128 * (j % 2) + 128]
-            v = al[h, :, 128 * j : 128 * (j + 1)].astype(F32) * g
+        for i in range(8):
+            g = 1.0 / gl[j, i // 2, :, 128 * (i % 2) : 128 * (i % 2) + 128]
+            v = al[j, :, 128 * i : 128 * (i + 1)].astype(F32) * g
             part = part + v * v
-        sqm[h, m] = lax.dot_general(
+        sqm[j, mj] = lax.dot_general(
             jnp.ones((8, 128), F32), part, NT, preferred_element_type=F32, precision=lax.Precision.HIGHEST
         )
         for e in around:
-            mi = (m + e) % 4
-            rc(sqm.at[h, m], sqm.at[h, m], sqS, sqR.at[h, m], dev(l, mi)).start()
-
-    def silu(v):
-        return v / (1.0 + jnp.exp(-v))
-
-    def hide(h):
-        for e in around:
-            mi = (m + e) % 4
-            arrived(sqm.at[h, mi], sqR.at[h, mi])
+            mi = (mj + e) % 4
+            rc(sqm.at[j, mj], sqm.at[j, mj], sqS, sqR.at[j, mj], devj(j, lj, mi)).start()
+
+    def hide(j):
+        lj, mj = places(j)
+        here = rows_of(mj, 64)
+        for e in around:
+            mi = (mj + e) % 4
+            arrived(sqm.at[j, mi], sqR.at[j, mi])
         total = lax.dot_general(
-            sqm[h, 0] + sqm[h, 1] + sqm[h, 2] + sqm[h, 3],
+            sqm[j, 0] + sqm[j, 1] + sqm[j, 2] + sqm[j, 3],
             (sub == 0).astype(F32),
             TN,
             preferred_element_type=F32,
             precision=lax.Precision.HIGHEST,
         )
         invs[...] = 1.0 / jnp.sqrt(total / MODEL_WIDTH + EPS)
-        inv = invs[my64, :]
-        for e in around:
-            mi = (m + e) % 4
-            arrived(rf.at[h, mi], rfR.at[h, mi])
+        inv = invs[here, :]
+        for e in around:
+            mi = (mj + e) % 4
+            arrived(rf.at[j, mi], rfR.at[j, mi])
 
         def tile(i):
             at = slice(128 * i, 128 * (i + 1))
-            v = pb[h, my64, at].astype(F32)
+            v = pb[j, here, at].astype(F32)
             for e in around:
-                v = v + rf[h, (m + e) % 4, :, at].astype(F32)
+                v = v + rf[j, (mj + e) % 4, :, at].astype(F32)
             return v * inv
 
         for i in range(3):
-            hb[h, my64, 128 * i : 128 * (i + 1)] = (silu(tile(i)) * tile(3 + i)).astype(BF)
+            hb[j, here, 128 * i : 128 * (i + 1)] = (silu(tile(i)) * tile(3 + i)).astype(BF)
         t = tile(6)
         low = lax.broadcasted_iota(jnp.int32, (64, 128), 1) < 64
-        hb[h, my64, 384:512] = jnp.where(low, silu(t) * pltpu.roll(t, 64, 1), 0.0).astype(BF)
-        for e in around:
-            rc(hb.at[h, my64, :], hb.at[h, my64, :], hS, hR.at[h, m], dev(l, (m + e) % 4)).start()
-
-    for h in halves:
-        gate(h)
-    for h in halves:
-        hide(h)
-
-    arrived(hb.at[0, pl.ds(0, 224), :], yS)
+        hb[j, here, 384:512] = jnp.where(low, silu(t) * pltpu.roll(t, 64, 1), 0.0).astype(BF)
+        for e in around:
+            rc(hb.at[j, here, :], hb.at[j, here, :], hS, hR.at[j, mj], devj(j, lj, (mj + e) % 4)).start()
+
+    gate(c)
+    arrived(wp.at[1 - c], swR)
+    gate(1 - c)
+    arrived(dwp.at[c, pl.ds(0, 448), :], dR)
+    rc(dwp.at[c, pl.ds(0, 448), :], dwp.at[c, pl.ds(0, 448), :], sdS, sdR, sibling).start()
+    for j in sets:
+        hide(j)
+
+    arrived(wp.at[c], swS)
+    arrived(mb.at[pl.ds(0, 192), :], yS)
     arrived(al.at[:, :, pl.ds(0, 768)], lS)
     arrived(pb.at[:, pl.ds(0, 192), :], rfS)
     arrived(sqm.at[:, pl.ds(0, 3)], sqS)
-    arrived(dwp.at[pl.ds(0, 448), pl.ds(0, 768)], dS)
-    arrived(dwp.at[pl.ds(0, 448), :], dR)
-
-    def down(h):
-        for e in around:
-            mi = (m + e) % 4
-            arrived(hb.at[h, rows_of(mi, 64), :], hR.at[h, mi])
-        yb[h] = dot(hb[h], dwp[...]).astype(BF)
-        for e in around:
-            to = (l + e) % 4
-            rc(yb.at[h, :, rows_of(to, COLS)], yr.at[h, l], oS, oR.at[h, l], dev(to, m)).start()
-
-    def finish(i, h):
-        v = yb[h, :, mycols].astype(F32)
-        for e in around:
-            lp = (l + e) % 4
-            arrived(yr.at[h, lp], oR.at[h, lp])
-            v = v + yr[h, lp].astype(F32)
-        fs[h] = v.astype(BF)
-        for e in around if i == 0 else (0,) + around:
-            yp = (y + e) % 4
-            rc(fs.at[h, rows_of(yp, 64), :], fb.at[k], fS, fR.at[k], (r, 2 * yp + h)).start()
-
-    for h in halves:
-        down(h)
-    for i, h in enumerate(halves):
-        finish(i, h)
+    arrived(dwp.at[c, pl.ds(0, 448), pl.ds(0, 768)], dS)
+
+    def down(j):
+        lj, mj = places(j)
+        for e in around:
+            mi = (mj + e) % 4
+            arrived(hb.at[j, rows_of(mi, 64), :], hR.at[j, mi])
+        yb[j] = dot(hb[j], dwp[j]).astype(BF)
+        for e in around:
+            to = (lj + e) % 4
+            rc(yb.at[j, :, rows_of(to, COLS)], yr.at[j, lj], oS, oR.at[j, lj], devj(j, to, mj)).start()
+
+    down(c)
+    arrived(dwp.at[1 - c, pl.ds(0, 448), :], sdR)
+    down(1 - c)
+    v = jnp.zeros((256, COLS), F32)
+    for j in sets:
+        lj, mj = places(j)
+        v = v + yb[j, :, rows_of(lj, COLS)].astype(F32)
+        for e in around:
+            lp = (lj + e) % 4
+            arrived(yr.at[j, lp], oR.at[j, lp])
+            v = v + yr[j, lp].astype(F32)
+    vf[...] = v
+    fs[...] = v.astype(BF)
+    for e in around:
+        yp = (y + e) % 4
+        rc(fs.at[rows_of(yp, 64), :], fb.at[y], fS, fR.at[y], (r, 2 * yp + c)).start()
     arrived(hb.at[:, pl.ds(0, 192), :], hS)
     arrived(yb.at[:, :, pl.ds(0, 768)], oS)
-    res = mid[...] + fs[c, mine, :].astype(F32)
-    for i, h in enumerate(halves):
-        for e in around if i == 0 else (0,) + around:
-            kp = 2 * ((y + e) % 4) + h
-            arrived(fb.at[kp], fR.at[kp])
-            res = res + fb[kp].astype(F32)
+    arrived(dwp.at[c, pl.ds(0, 448), :], sdS)
+    res = mid[...] + vf[mine, :]
+    for e in around:
+        yp = (y + e) % 4
+        arrived(fb.at[yp], fR.at[yp])
+        res = res + fb[yp].astype(F32)
     out[...] = res.astype(BF)
-    arrived(yb.at[0, pl.ds(0, 112), :], fS)
+    arrived(fs.at[pl.ds(0, 192), :], fS)
 
 
 def shards(
@@ -431,9 +452,9 @@
             V((2, COLS, 128), BF),
             V((2, COLS, 128), BF),
             V((4, COLS, 128), BF),
-            V((1024, CHUNK), BF),
-            V((512, 1024), BF),
-            V((4, 1, COLS), F32),
+            V((2, 1024, CHUNK), BF),
+            V((2, 512, 1024), BF),
+            V((2, 4, 1, COLS), F32),
             V((2, 256, 1024), BF),
             V((64, COLS), F32),
             V((2, 256, CHUNK), BF),
@@ -441,10 +462,12 @@
             V((2, 256, 512), BF),
             V((2, 256, 1024), BF),
             V((2, 4, 256, COLS), BF),
-            V((2, 256, COLS), BF),
-            V((NK, 64, COLS), BF),
+            V((256, COLS), F32),
+            V((256, COLS), BF),
+            V((4, 64, COLS), BF),
             V((256, 128), F32),
             V((2, 4, 8, 256), F32),
+            V((256, COLS), BF),
             dma(11),
             dma(),
             dma(),
@@ -452,14 +475,14 @@
             dma(),
             dma(),
             dma(),
-            dma(3),
+            dma(2, 3),
+            dma(2, 4),
+            dma(),
+            dma(),
+            pltpu.SemaphoreType.REGULAR,
+            dma(),
             dma(4),
             dma(),
-            dma(),
-            pltpu.SemaphoreType.REGULAR,
-            dma(),
-            dma(NK),
-            dma(),
             dma(2, 4),
             dma(),
             dma(2, 4),
@@ -470,7 +493,11 @@
             dma(),
             dma(2, 4),
             dma(),
-            dma(NK),
+            dma(4),
+            dma(),
+            dma(),
+            dma(),
+            dma(),
         ],
         compiler_params=pltpu.CompilerParams(
             collective_id=0, has_side_effects=True, vmem_limit_bytes=56 << 20

time: 77.5 us -> 74.9 us (0.966)
  the two profiles are of different devices: /device:TPU:1 before, /device:TPU:0 now
where the time goes in v4:
time: 74.9 us; the launch traced here: 74.7 us
  Pallas kernels  73.3 us (98%)
  local copies, waits for them, and re-layouts  1.38 us (2%)
    pallas_call x1, Pallas kernels, shards(): pl.pallas_call(kernel, out_shape=jax.ShapeDtypeStruct((64, COLS), BF), in...  73.3 us

profile of v4, /device:TPU:0, one launch (start us, length us, event | category | flops | bytes accessed | tf_op | source)
XLA Modules:
  0.0 74.7 jit_solution(1913158159666449515)
XLA Ops:
  0.0 73.3 %shard_map.136 = bf16[64,256]{1,0:T(8,128)(2,1)} custom-call(s32[32]{0:T(128)} %lens.1, s32[1,32]{1,0:T(1,128)} %bitcast.9, bf16[512,256]{1,0:T(8,128)(2,1)} %resid.1, f32[1,4096]{1,0:T(1,128)} %bitcast.7, bf16[4096,512]{1,0:T(8,128)(2,1)} %wq.1, bf16[4096,128]{1,0:T(8,128)(2,1)} %wk.1, bf16[4096,128]{1,0:T(8,128)(2,1)} %wv.1, ...), custom_call_target="tpu_custom_call" | custom-call | tf_op jit(solution)/shard_map/pallas_call | solution.py:429
  73.3 1.4 %copy.16 = bf16[64,256]{1,0:T(8,128)(2,1)} copy(bf16[64,256]{1,0:T(8,128)(2,1)} %shard_map.136) | data formatting | bytes 65536

commit v5 on v4

--- a/solution.py
+++ b/solution.py
@@ -95,10 +95,6 @@
     load("wq", wq, wq_v)
     load("wk", wk, wk_v)
     load("wv", wv, wv_v)
-    load("kc", kc, k_v)
-    load("vc", vc, v_v)
-    load("wo", wo, wo_v)
-    load("res", resid.at[rows_of(k, 64), :], res_v)
 
     pl.semaphore_wait(barrier, NR - 1 + NK - 1)
 
@@ -107,6 +103,8 @@
         rc(resid.at[rows_of(to, ROWS), :], tok.at[:, rows_of(r, COLS)], tokS, tokR, (to, k)).start()
     for d in range(1, NK):
         pl.semaphore_signal(b2, inc=1, device_id=(r, (k + d) % NK), device_id_type=MESH)
+
+    load("kc", kc, k_v)
 
     def w_copies(d):
         to = (l + d) % 4
@@ -157,6 +155,7 @@
                 out.append(rc(gain2, gl.at[j, lj], gS.at[j, d - 1], gR.at[j, lj], to))
         return out
 
+    load("vc", vc, v_v)
     for j in range(2):
         gl[j, places(j)[0]] = gain2[...]
     for copy in gain_copies():
@@ -167,6 +166,9 @@
     v3[...] = jnp.zeros_like(v3)
     for j in range(2):
         dwp[j, 448:512, :] = jnp.zeros((64, 1024), BF)
+
+    load("wo", wo, wo_v)
+    load("res", resid.at[rows_of(k, 64), :], res_v)
 
     sub = lax.broadcasted_iota(jnp.int32, (8, 128), 0)
     lane = lax.broadcasted_iota(jnp.int32, (ROWS, HD), 1)
@@ -203,6 +205,7 @@
     factor = 1.0 / math.sqrt(HD)
     slot = lax.broadcasted_iota(jnp.int32, (8, SLOTS), 1)
     loads["kc"].wait()
+    kd = r // 2
     for half in range(2):
         for b in range(16 * half, 16 * half + 16):
             rows = slice(8 * b, 8 * b + 8)
@@ -224,23 +227,25 @@
         for b in range(16 * half, 16 * half + 16):
             rows = slice(8 * b, 8 * b + 8)
             o3[rows, :] += dot(w3[rows, :].astype(BF), v_v[b])
-    for h in range(HEADS):
-        att[:, HD * h : HD * (h + 1)] = o3[pl.ds(h, ROWS, stride=8), :].astype(BF)
-
-    kd = r // 2
-    there = attb.at[rows_of(r % 2, ROWS), rows_of(k, 512)]
-    pl.semaphore_wait(b2, NK - 1)
-
-    @pl.when(k == kd)
-    def _():
-        pltpu.make_async_copy(att, there, attR).start()
-
-    @pl.when(k != kd)
-    def _():
-        rc(att, there, attS, attR, (r, kd)).start()
-
-    for d in range(1, NR):
-        rc(att, there, attS, attR, ((r + d) % NR, kd)).start()
+        ours = slice(16 * half, 16 * half + 16)
+        for h in range(HEADS):
+            att[ours, HD * h : HD * (h + 1)] = o3[pl.ds(128 * half + h, 16, stride=8), :].astype(BF)
+
+        block = att.at[ours, :]
+        there = attb.at[pl.ds(pl.multiple_of(ROWS * (r % 2) + 16 * half, 16), 16), rows_of(k, 512)]
+        if half == 0:
+            pl.semaphore_wait(b2, NK - 1)
+
+        @pl.when(k == kd)
+        def _():
+            pltpu.make_async_copy(block, there, attR).start()
+
+        @pl.when(k != kd)
+        def _():
+            rc(block, there, attS, attR, (r, kd)).start()
+
+        for d in range(1, NR):
+            rc(block, there, attS, attR, ((r + d) % NR, kd)).start()
 
     arrived(tok.at[:, pl.ds(0, COLS * 15)], tokS)
     arrived(wp.at[c, pl.ds(0, 768), :], wS)
@@ -250,11 +255,6 @@
     loads["wo"].wait()
     loads["res"].wait()
     arrived(attb, attR)
-    for d in (1, 3, 2, 0):
-        for copy in d_copies(d):
-            copy.start()
-    arrived(wp.at[c], wR)
-    rc(wp.at[c], wp.at[c], swS, swR, sibling).start()
     o = res_v[...].astype(F32) + dot(attb[...], wo_v[...])
     mid[...] = o
     mine = rows_of(y, 64)
@@ -279,6 +279,11 @@
             if i == 0:
                 arrived(mb.at[rows_of(yp, 64), :], yR.at[yp])
             line_sends(j, yp)
+    arrived(wp.at[c], wR)
+    rc(wp.at[c], wp.at[c], swS, swR, sibling).start()
+    for d in (1, 3, 2, 0):
+        for copy in d_copies(d):
+            copy.start()
     for j in range(2):
         al[j, :, rows_of(places(j)[0], COLS)] = mb[...]
 

time: 74.9 us -> 73.1 us (0.976)
  Pallas kernels: 73.3 us -> 71.5 us
    pallas_call x1, Pallas kernels: 73.3 us -> 71.5 us  [shards(): pl.pallas_call(kernel, out_shape=jax.ShapeDtypeStruct((64, COLS), BF), in...]
where the time goes in v5:
time: 73.1 us; the launch traced here: 72.9 us
  Pallas kernels  71.5 us (98%)
  local copies, waits for them, and re-layouts  1.38 us (2%)
    pallas_call x1, Pallas kernels, shards(): pl.pallas_call(kernel, out_shape=jax.ShapeDtypeStruct((64, COLS), BF), in...  71.5 us

profile of v5, /device:TPU:0, one launch (start us, length us, event | category | flops | bytes accessed | tf_op | source)
XLA Modules:
  0.0 72.9 jit_solution(886544184886973175)
XLA Ops:
  0.0 71.5 %shard_map.136 = bf16[64,256]{1,0:T(8,128)(2,1)} custom-call(s32[32]{0:T(128)} %lens.1, s32[1,32]{1,0:T(1,128)} %bitcast.9, bf16[512,256]{1,0:T(8,128)(2,1)} %resid.1, f32[1,4096]{1,0:T(1,128)} %bitcast.7, bf16[4096,512]{1,0:T(8,128)(2,1)} %wq.1, bf16[4096,128]{1,0:T(8,128)(2,1)} %wk.1, bf16[4096,128]{1,0:T(8,128)(2,1)} %wv.1, ...), custom_call_target="tpu_custom_call" | custom-call | tf_op jit(solution)/shard_map/pallas_call | solution.py:434
  71.5 1.4 %copy.16 = bf16[64,256]{1,0:T(8,128)(2,1)} copy(bf16[64,256]{1,0:T(8,128)(2,1)} %shard_map.136) | data formatting | bytes 65536

commit v6 on v5

--- a/solution.py
+++ b/solution.py
@@ -39,8 +39,9 @@
 
 
 def kernel(
-    lens, pos, resid, gain1, wq, wk, wv, kc, vc, wo, gain2, gw, uw, dw,
+    lens_h, pos_h, resid, gain1_h, wq, wk, wv, kc, vc, wo, gain2_h, gw, uw, dw,
     out,
+    lens, pos, gain1, gain2,
     tok, nrm, wq_v, wk_v, wv_v, k_v, v_v, q3, k3, v3, o3, s3, w3, att, attb, wo_v, res_v,
     gp, up, pk, wp, dwp, gl, al, mid, pb, rf, hb, yb, yr, vf, fs, fb, invs, sqm, mb,
     ld, tokS, tokR, wS, wR, dS, dR, gS, gR, attS, attR, b2, yS, yR, lS, alR, sqS, sqR,
@@ -92,6 +93,10 @@
     load("g10", gw.at[:, pl.ds(1280, 128)], gp.at[1])
     load("u3", uw.at[:, pl.ds(384, 128)], up.at[0])
     load("u10", uw.at[:, pl.ds(1280, 128)], up.at[1])
+    load("gain2", gain2_h, gain2)
+    load("gain1", gain1_h, gain1)
+    load("lens", lens_h, lens)
+    load("pos", pos_h, pos)
     load("wq", wq, wq_v)
     load("wk", wk, wk_v)
     load("wv", wv, wv_v)
@@ -156,6 +161,7 @@
         return out
 
     load("vc", vc, v_v)
+    loads["gain2"].wait()
     for j in range(2):
         gl[j, places(j)[0]] = gain2[...]
     for copy in gain_copies():
@@ -170,6 +176,9 @@
     load("wo", wo, wo_v)
     load("res", resid.at[rows_of(k, 64), :], res_v)
 
+    loads["pos"].wait()
+    loads["lens"].wait()
+    loads["gain1"].wait()
     sub = lax.broadcasted_iota(jnp.int32, (8, 128), 0)
     lane = lax.broadcasted_iota(jnp.int32, (ROWS, HD), 1)
     p8 = jnp.broadcast_to(pos[...].astype(F32), (8, ROWS))
@@ -210,7 +219,7 @@
         for b in range(16 * half, 16 * half + 16):
             rows = slice(8 * b, 8 * b + 8)
             s = lax.dot_general(q3[rows, :].astype(BF), k_v[b], NT, preferred_element_type=F32)
-            n = lens[b]
+            n = lens[0, b]
             ok = (slot < n) & ((slot < SINKS) | (slot > n - WINDOW))
             s3[rows, :] = jnp.where(ok, s * factor, -1e30)
         rows = slice(128 * half, 128 * half + 128)
@@ -238,14 +247,14 @@
 
         @pl.when(k == kd)
         def _():
-            pltpu.make_async_copy(block, there, attR).start()
+            pltpu.make_async_copy(block, there, attR.at[k]).start()
 
         @pl.when(k != kd)
         def _():
-            rc(block, there, attS, attR, (r, kd)).start()
+            rc(block, there, attS, attR.at[k], (r, kd)).start()
 
         for d in range(1, NR):
-            rc(block, there, attS, attR, ((r + d) % NR, kd)).start()
+            rc(block, there, attS, attR.at[k], ((r + d) % NR, kd)).start()
 
     arrived(tok.at[:, pl.ds(0, COLS * 15)], tokS)
     arrived(wp.at[c, pl.ds(0, 768), :], wS)
@@ -254,13 +263,16 @@
 
     loads["wo"].wait()
     loads["res"].wait()
-    arrived(attb, attR)
-    o = res_v[...].astype(F32) + dot(attb[...], wo_v[...])
+    o = res_v[...].astype(F32)
+    for d in (0, 1, 2, 3, 6, 7, 4, 5):
+        kp = 2 * ((y + d // 2) % 4) + (c + d % 2) % 2
+        arrived(attb.at[:, rows_of(kp, 512)], attR.at[kp])
+        o = o + dot(attb[:, rows_of(kp, 512)], wo_v[rows_of(kp, 512), :])
     mid[...] = o
     mine = rows_of(y, 64)
     mb[mine, :] = (o * gain2[...]).astype(BF)
 
-    around = (1, 3, 2)
+    around = (2, 1, 3)
     sets = (c, 1 - c)
 
     def line_sends(j, yp):
@@ -428,15 +440,18 @@
 ):
     hbm = pl.BlockSpec(memory_space=pltpu.MemorySpace.HBM)
     vmem = pl.BlockSpec(memory_space=pltpu.MemorySpace.VMEM)
-    smem = pl.BlockSpec(memory_space=pltpu.MemorySpace.SMEM)
     V = pltpu.VMEM
     dma = lambda *shape: pltpu.SemaphoreType.DMA(shape) if shape else pltpu.SemaphoreType.DMA
     return pl.pallas_call(
         kernel,
         out_shape=jax.ShapeDtypeStruct((64, COLS), BF),
-        in_specs=[smem, vmem, hbm, vmem, hbm, hbm, hbm, hbm, hbm, hbm, vmem, hbm, hbm, hbm],
+        in_specs=[hbm] * 14,
         out_specs=vmem,
         scratch_shapes=[
+            pltpu.SMEM((1, ROWS), jnp.int32),
+            V((1, ROWS), jnp.int32),
+            V((1, MODEL_WIDTH), F32),
+            V((1, COLS), F32),
             V((ROWS, MODEL_WIDTH), BF),
             V((ROWS, MODEL_WIDTH), BF),
             V((MODEL_WIDTH, HEADS * HD), BF),
@@ -473,7 +488,7 @@
             V((256, 128), F32),
             V((2, 4, 8, 256), F32),
             V((256, COLS), BF),
-            dma(11),
+            dma(15),
             dma(),
             dma(),
             dma(),
@@ -483,7 +498,7 @@
             dma(2, 3),
             dma(2, 4),
             dma(),
-            dma(),
+            dma(NK),
             pltpu.SemaphoreType.REGULAR,
             dma(),
             dma(4),
@@ -508,7 +523,7 @@
             collective_id=0, has_side_effects=True, vmem_limit_bytes=56 << 20
         ),
     )(
-        cache_lengths,
+        cache_lengths.reshape(1, ROWS),
         positions.reshape(1, ROWS),
         residual_in,
         attn_gain.reshape(1, MODEL_WIDTH),

time: 73.1 us -> 70.8 us (0.969)
  Pallas kernels: 71.5 us -> 69.2 us
    pallas_call x1, Pallas kernels: 71.5 us -> 69.2 us  [shards(): pl.pallas_call(kernel, out_shape=jax.ShapeDtypeStruct((64, COLS), BF), in...]
where the time goes in v6:
time: 70.8 us; the launch traced here: 70.6 us
  Pallas kernels  69.2 us (98%)
  local copies, waits for them, and re-layouts  1.38 us (2%)
    pallas_call x1, Pallas kernels, shards(): pl.pallas_call(kernel, out_shape=jax.ShapeDtypeStruct((64, COLS), BF), in...  69.2 us

profile of v6, /device:TPU:0, one launch (start us, length us, event | category | flops | bytes accessed | tf_op | source)
XLA Modules:
  0.0 70.6 jit_solution(929953775340387429)
XLA Ops:
  0.0 69.2 %shard_map.136 = bf16[64,256]{1,0:T(8,128)(2,1)} custom-call(s32[1,32]{1,0:T(1,128)} %bitcast.10, s32[1,32]{1,0:T(1,128)} %bitcast.11, bf16[512,256]{1,0:T(8,128)(2,1)} %resid.1, f32[1,4096]{1,0:T(1,128)} %bitcast.8, bf16[4096,512]{1,0:T(8,128)(2,1)} %wq.1, bf16[4096,128]{1,0:T(8,128)(2,1)} %wk.1, bf16[4096,128]{1,0:T(8,128)(2,1)} %wv.1, ...), custom_call_target="tpu_custom_call" | custom-call | tf_op jit(solution)/shard_map/pallas_call | solution.py:445
  69.2 1.4 %copy.16 = bf16[64,256]{1,0:T(8,128)(2,1)} copy(bf16[64,256]{1,0:T(8,128)(2,1)} %shard_map.136) | data formatting | bytes 65536

commit v7 on v6

--- a/solution.py
+++ b/solution.py
@@ -97,12 +97,12 @@
     load("gain1", gain1_h, gain1)
     load("lens", lens_h, lens)
     load("pos", pos_h, pos)
+
+    pl.semaphore_wait(barrier, NR - 1 + NK - 1)
+
     load("wq", wq, wq_v)
     load("wk", wk, wk_v)
     load("wv", wv, wv_v)
-
-    pl.semaphore_wait(barrier, NR - 1 + NK - 1)
-
     for d in range(1, NR):
         to = (r + d) % NR
         rc(resid.at[rows_of(to, ROWS), :], tok.at[:, rows_of(r, COLS)], tokS, tokR, (to, k)).start()
@@ -138,7 +138,7 @@
         return [rc(s, t, dS, dR, dev(to, m)) for s, t in pieces]
 
     w_sends = {d: w_copies(d) for d in range(4)}
-    for d in (1, 3, 2, 0):
+    for d in (2, 1, 3, 0):
         w_sends[d][0].start()
         w_sends[d][1].start()
     for name in ("g3", "g10", "u3", "u10"):
@@ -256,11 +256,6 @@
         for d in range(1, NR):
             rc(block, there, attS, attR.at[k], ((r + d) % NR, kd)).start()
 
-    arrived(tok.at[:, pl.ds(0, COLS * 15)], tokS)
-    arrived(wp.at[c, pl.ds(0, 768), :], wS)
-    for copy in gain_copies():
-        copy.wait_send()
-
     loads["wo"].wait()
     loads["res"].wait()
     o = res_v[...].astype(F32)
@@ -372,11 +367,15 @@
     gate(c)
     arrived(wp.at[1 - c], swR)
     gate(1 - c)
+    for j in sets:
+        hide(j)
     arrived(dwp.at[c, pl.ds(0, 448), :], dR)
     rc(dwp.at[c, pl.ds(0, 448), :], dwp.at[c, pl.ds(0, 448), :], sdS, sdR, sibling).start()
-    for j in sets:
-        hide(j)
-
+
+    arrived(tok.at[:, pl.ds(0, COLS * 15)], tokS)
+    arrived(wp.at[c, pl.ds(0, 768), :], wS)
+    for copy in gain_copies():
+        copy.wait_send()
     arrived(wp.at[c], swS)
     arrived(mb.at[pl.ds(0, 192), :], yS)
     arrived(al.at[:, :, pl.ds(0, 768)], lS)

time: 70.8 us -> 70.6 us (level)
  no operation moved by 1% of the time
where the time goes in v7:
time: 70.6 us; the launch traced here: 70.4 us
  Pallas kernels  69.1 us (98%)
  local copies, waits for them, and re-layouts  1.38 us (2%)
    pallas_call x1, Pallas kernels, shards(): pl.pallas_call(kernel, out_shape=jax.ShapeDtypeStruct((64, COLS), BF), in...  69.1 us

profile of v7, /device:TPU:0, one launch (start us, length us, event | category | flops | bytes accessed | tf_op | source)
XLA Modules:
  0.0 70.4 jit_solution(14200182304435839144)
XLA Ops:
  0.0 69.1 %shard_map.136 = bf16[64,256]{1,0:T(8,128)(2,1)} custom-call(s32[1,32]{1,0:T(1,128)} %bitcast.10, s32[1,32]{1,0:T(1,128)} %bitcast.11, bf16[512,256]{1,0:T(8,128)(2,1)} %resid.1, f32[1,4096]{1,0:T(1,128)} %bitcast.8, bf16[4096,512]{1,0:T(8,128)(2,1)} %wq.1, bf16[4096,128]{1,0:T(8,128)(2,1)} %wk.1, bf16[4096,128]{1,0:T(8,128)(2,1)} %wv.1, ...), custom_call_target="tpu_custom_call" | custom-call | tf_op jit(solution)/shard_map/pallas_call | solution.py:444
  69.1 1.4 %copy.16 = bf16[64,256]{1,0:T(8,128)(2,1)} copy(bf16[64,256]{1,0:T(8,128)(2,1)} %shard_map.136) | data formatting | bytes 65536
